TPU v7x, 32 devices: a whole 2x2x4 slice. The times are simulated.
32 devices in a mesh: shard: 8 (over z, y), tensor: 4 (over x, core).
Axes of the slice: x: 2, y: 2, z: 4, core: 2. Of those that a mesh axis runs over, the one named last changes fastest.
Arguments:
- tokens: bfloat16 [12608, 1024], P('shard'), may hold values from -6 to 6
- cotangent: bfloat16 [12608, 1024], P('shard'), may hold values from -6 to 6
- input_weight: float32 [3, 1024, 1024], P(None, 'shard', 'tensor'), may hold values from -2 to 2
- input_moments: float32 [2, 3, 1024, 1024], P(None, None, 'shard', 'tensor'), may hold values from -1 to 1, as said below
- input_bias: float32 [2, 1024], P(None, ('tensor', 'shard')), may hold values from -3 to 3
- input_bias_moments: float32 [2, 2, 1024], P(None, None, ('tensor', 'shard')), may hold values from -1 to 1, as said below
- output_weight: float32 [1024, 1024], P('tensor', 'shard'), may hold values from -0.75 to 0.75
- output_moments: float32 [2, 1024, 1024], P(None, 'tensor', 'shard'), may hold values from -1 to 1, as said below
- expand_weight: float32 [1024, 4096], P('shard', 'tensor'), may hold values from -0.1875 to 0.1875
- expand_moments: float32 [2, 1024, 4096], P(None, 'shard', 'tensor'), may hold values from -1 to 1, as said below
- expand_bias: float32 [4096], P(('tensor', 'shard')), may hold values from -3 to 3
- expand_bias_moments: float32 [2, 4096], P(None, ('tensor', 'shard')), may hold values from -1 to 1, as said below
- shrink_weight: float32 [4096, 1024], P('tensor', 'shard'), may hold values from -0.09375 to 0.09375
- shrink_moments: float32 [2, 4096, 1024], P(None, 'tensor', 'shard'), may hold values from -1 to 1, as said below
- vectors: float32 [6, 1024], P(None, 'shard'), may hold values from -1.2 to 1.4
- vector_moments: float32 [2, 6, 1024], P(None, None, 'shard'), may hold values from -1 to 1, as said below
Outputs:
- block_output: bfloat16 [12608, 1024], P('shard')
- token_gradient: float32 [12608, 1024], P('shard')
- input_weight_gradient: float32 [3, 1024, 1024], P(None, 'shard', 'tensor')
- input_bias_gradient: float32 [2, 1024], P(None, ('tensor', 'shard'))
- output_weight_gradient: float32 [1024, 1024], P('tensor', 'shard')
- expand_weight_gradient: float32 [1024, 4096], P('shard', 'tensor')
- expand_bias_gradient: float32 [4096], P(('tensor', 'shard'))
- shrink_weight_gradient: float32 [4096, 1024], P('tensor', 'shard')
- vectors_gradient: float32 [6, 1024], P(None, 'shard')
- new_input_weight: float32 [3, 1024, 1024], P(None, 'shard', 'tensor')
- new_input_bias: float32 [2, 1024], P(None, ('tensor', 'shard'))
- new_output_weight: float32 [1024, 1024], P('tensor', 'shard')
- new_expand_weight: float32 [1024, 4096], P('shard', 'tensor')
- new_expand_bias: float32 [4096], P(('tensor', 'shard'))
- new_shrink_weight: float32 [4096, 1024], P('tensor', 'shard')
- new_vectors: float32 [6, 1024], P(None, 'shard')
- new_input_moments: float32 [2, 3, 1024, 1024], P(None, None, 'shard', 'tensor')
- new_input_bias_moments: float32 [2, 2, 1024], P(None, None, ('tensor', 'shard'))
- new_output_moments: float32 [2, 1024, 1024], P(None, 'tensor', 'shard')
- new_expand_moments: float32 [2, 1024, 4096], P(None, 'shard', 'tensor')
- new_expand_bias_moments: float32 [2, 4096], P(None, ('tensor', 'shard'))
- new_shrink_moments: float32 [2, 4096, 1024], P(None, 'tensor', 'shard')
- new_vector_moments: float32 [2, 6, 1024], P(None, None, 'shard')
Inputs may be any that keep to these rules, and one draw needn't show every extreme that they name: `input_moments`: second moments positive. `input_bias_moments`: second moments positive. `output_moments`: second moments positive. `expand_moments`: second moments positive. `expand_bias_moments`: second moments positive. `shrink_moments`: second moments positive. `vector_moments`: second moments positive.
All inputs are finite; a program needn't handle non-finite values.
Results may differ from a plain program's by a relative error of at most 0.015.
Values may be sent and summed in bfloat16 or wider, within the bound.
No kernel may reach another device: no remote copies, remote signals or barrier semaphores. Data moves between devices by JAX's collectives and lax.ppermute only.
A program may use at most 192 MiB of HBM per device.

v0:
```python
import functools

import jax
import jax.numpy as jnp
from jax import lax
from jax.experimental import pallas as pl
from jax.experimental.pallas import tpu as pltpu
from jax.sharding import PartitionSpec as P


HEAD = 64
SEQ = 197
PAD = 208
LANES = 128
SHARD, TENSOR = "shard", "tensor"

norm_eps = 1e-06
rate = 0.003
first_decay = 0.9
second_decay = 0.95
weight_decay = 0.05
step_count = 2.0
adam_eps = 1e-08
loss_scale = 128.0


bf16 = jnp.bfloat16
f32 = jnp.float32
NT = (((1,), (1,)), ((), ()))
TN = (((0,), (0,)), ((), ()))
PARAMS = pltpu.CompilerParams(vmem_limit_bytes=40 * 1024 * 1024)


def dot(left, right):
    return jnp.dot(left, right, preferred_element_type=f32)


def dot_nt(left, right):
    return lax.dot_general(left, right, NT, preferred_element_type=f32)


def dot_tn(left, right):
    return lax.dot_general(left, right, TN, preferred_element_type=f32)


def whole(shape):
    return pl.BlockSpec(shape, lambda i, idx: (0,) * len(shape))


def picked(shape):
    return pl.BlockSpec((1,) + shape, lambda i, idx: (idx[i],) + (0,) * len(shape))


def store_one(refs, i, value):
    for j, ref in enumerate(refs):

        @pl.when(i == j)
        def _():
            ref[...] = value


def load_one(refs, i, scratch):
    for j, ref in enumerate(refs):

        @pl.when(i == j)
        def _():
            scratch[...] = ref[...]

    return scratch[...]


def norm_stats(values):
    centred = values - jnp.mean(values, axis=-1, keepdims=True)
    spread = jnp.mean(centred * centred, axis=-1, keepdims=True)
    inverse = lax.rsqrt(spread + norm_eps)
    return centred * inverse, inverse


def norm_back(unit, inverse, grad, gain):
    scaled = grad * gain
    mean_one = jnp.mean(scaled, axis=-1, keepdims=True)
    mean_two = jnp.mean(scaled * unit, axis=-1, keepdims=True)
    return inverse * (scaled - mean_one - unit * mean_two)


def attn_fwd_kernel(width, shared, idx, tok, w, vec, bias, *rest):
    rest = rest[shared:]
    inputs_out, qkv_out, ctx_out = rest[:3]
    parts = rest[3:]
    i = pl.program_id(0)
    unit, _ = norm_stats(tok[0].astype(f32))
    inputs = (unit * vec[0:1, :] + vec[1:2, :]).astype(bf16)
    inputs_out[0] = inputs
    project = dot(inputs, w[:, : 3 * width])
    query = (project[:, :width] + bias[0:1, :]).astype(bf16)
    keys = project[:, width : 2 * width].astype(bf16)
    values = (project[:, 2 * width :] + bias[1:2, :]).astype(bf16)
    qkv_out[0, :, :width] = query
    qkv_out[0, :, width : 2 * width] = keys
    qkv_out[0, :, 2 * width :] = values
    scale = bf16(HEAD ** (-0.5))
    lane = lax.broadcasted_iota(jnp.int32, (1, LANES), 1)
    live = lax.broadcasted_iota(jnp.int32, (1, PAD), 1) < SEQ

    def one_image(image, _):
        rows = pl.ds(pl.multiple_of(image * PAD, PAD), PAD)
        for pair in range(width // LANES):
            at = [slice(c * width + pair * LANES, c * width + (pair + 1) * LANES) for c in range(3)]
            q2, k2, v2 = qkv_out[0, rows, at[0]] * scale, qkv_out[0, rows, at[1]], qkv_out[0, rows, at[2]]
            outs = []
            for half in range(LANES // HEAD):
                mine = (lane // HEAD) == half
                scores = dot_nt(jnp.where(mine, q2, bf16(0)), k2)
                scores = jnp.where(live, scores, -1e30)
                raised = jnp.exp(scores - jnp.max(scores, axis=-1, keepdims=True))
                total = jnp.sum(raised, axis=-1, keepdims=True)
                outs.append(dot((raised * (1.0 / total)).astype(bf16), v2))
            ctx_out[0, rows, at[0]] = jnp.where(lane < HEAD, outs[0], outs[1]).astype(bf16)
        return 0

    lax.fori_loop(0, tok.shape[1] // PAD, one_image, 0)
    store_one(parts, i, dot_nt(ctx_out[0], w[:, 3 * width : 4 * width]).astype(bf16))


def ffn_kernel(nq, shared, idx, *refs):
    pieces, (cot, w, bias) = refs[:nq], refs[nq : nq + 3]
    refs = refs[nq + 3 + shared :]
    x_out, hid_out, pre_out, bias_out = refs[:4]
    shrink_parts, mid_parts, scratch = refs[4 : 4 + nq], refs[4 + nq : 4 + 2 * nq], refs[-1]
    i = pl.program_id(0)
    width = bias.shape[1]
    x = load_one(pieces, i, scratch)
    x_out[0] = x
    back = cot[0]

    @pl.when(i == 0)
    def _():
        bias_out[...] = jnp.zeros_like(bias_out)

    step = 512

    def some_columns(k, _):
        start = pl.multiple_of(k * step, step)
        cols, second = pl.ds(start, step), pl.ds(width + start, step)
        pre = dot(x, w[:, cols]) + bias[0:1, cols]
        grad = dot(back, w[:, second])
        share = 0.5 + 0.5 * lax.erf(pre * (0.5**0.5))
        slope = share + pre * (jnp.exp(-0.5 * pre * pre) * 0.3989422804014327)
        hid_out[0, :, cols] = (pre * share).astype(bf16)
        pre_grad = (slope * grad).astype(bf16)
        pre_out[0, :, cols] = pre_grad
        bias_out[0:1, cols] += jnp.sum(pre_grad.astype(f32), axis=0, keepdims=True)
        return 0

    lax.fori_loop(0, width // step, some_columns, 0)
    store_one(shrink_parts, i, dot_nt(hid_out[0], w[:, width:]).astype(bf16))
    store_one(mid_parts, i, dot_nt(pre_out[0], w[:, :width]).astype(bf16))


def attn_bwd_kernel(nq, width, shared, idx, *refs):
    pieces, (tok, qkv, w) = refs[:nq], refs[nq : nq + 3]
    refs = refs[nq + 3 + shared :]
    mid_out, grad_out, sums_out, vec_out = refs[:4]
    parts, scratch, ctx_grads = refs[4 : 4 + nq], refs[-2], refs[-1]
    i = pl.program_id(0)
    mid = load_one(pieces, i, scratch)
    mid_out[0] = mid
    ctx_grad = dot(mid, w[:, 3 * width : 4 * width]).astype(bf16)
    scale = bf16(HEAD ** (-0.5))
    lane = lax.broadcasted_iota(jnp.int32, (1, LANES), 1)
    live = lax.broadcasted_iota(jnp.int32, (PAD, 1), 0) < SEQ

    ctx_grads[...] = ctx_grad

    def one_image(image, _):
        rows = pl.ds(pl.multiple_of(image * PAD, PAD), PAD)
        for pair in range(width // LANES):
            at = [slice(c * width + pair * LANES, c * width + (pair + 1) * LANES) for c in range(3)]
            q2, k2, v2 = qkv[0, rows, at[0]] * scale, qkv[0, rows, at[1]], qkv[0, rows, at[2]]
            c2 = ctx_grads[rows, pair * LANES : (pair + 1) * LANES]
            outs = []
            for half in range(LANES // HEAD):
                mine = (lane // HEAD) == half
                scores = dot_nt(k2, jnp.where(mine, q2, bf16(0)))
                scores = jnp.where(live, scores, -1e30)
                raised = jnp.exp(scores - jnp.max(scores, axis=0, keepdims=True))
                prob = raised * (1.0 / jnp.sum(raised, axis=0, keepdims=True))
                prob_grad = dot_nt(v2, jnp.where(mine, c2, bf16(0)))
                row_dot = jnp.sum(prob_grad * prob, axis=0, keepdims=True)
                score_grad = (prob * (prob_grad - row_dot)).astype(bf16)
                outs.append(
                    (
                        dot_tn(score_grad, k2) * HEAD ** (-0.5),
                        dot(score_grad, q2),
                        dot(prob.astype(bf16), c2),
                    )
                )
            for c in range(3):
                grad_out[0, rows, at[c]] = jnp.where(lane < HEAD, outs[0][c], outs[1][c]).astype(bf16)
        return 0

    lax.fori_loop(0, tok.shape[1] // PAD, one_image, 0)
    grads = grad_out[0]
    part = dot_nt(grads, w[:, : 3 * width])
    store_one(parts, i, part.astype(bf16))
    unit, _ = norm_stats(tok[0].astype(f32))

    @pl.when(i == 0)
    def _():
        sums_out[...] = jnp.zeros_like(sums_out)
        vec_out[...] = jnp.zeros_like(vec_out)

    sums_out[0:1, :] += jnp.sum(grads.astype(f32), axis=0, keepdims=True)
    vec_out[0:1, :] += jnp.sum(part * unit, axis=0, keepdims=True)
    vec_out[1:2, :] += jnp.sum(part, axis=0, keepdims=True)


def mid_kernel(idx, tok, mine, theirs, vec, attended_out, normed_out):
    attended = tok[0].astype(f32) + (mine[...].astype(f32) + theirs[...].astype(f32)) + vec[2:3, :]
    attended_out[...] = attended
    unit, _ = norm_stats(attended)
    normed_out[...] = (unit * vec[3:4, :] + vec[4:5, :]).astype(bf16)


def mid_back_kernel(idx, attended, cot, mine, theirs, vec, mid_out, low_out, sums_out):
    grad = mine[...].astype(f32) + theirs[...].astype(f32)
    unit, inverse = norm_stats(attended[...])
    back = cot[0].astype(f32)
    mid = back + norm_back(unit, inverse, grad, vec[3:4, :])
    mid_out[...] = mid
    low_out[...] = mid.astype(bf16)

    @pl.when(pl.program_id(0) == 0)
    def _():
        sums_out[...] = jnp.zeros_like(sums_out)

    sums_out[0:1, :] += jnp.sum(mid, axis=0, keepdims=True)
    sums_out[1:2, :] += jnp.sum(grad * unit, axis=0, keepdims=True)
    sums_out[2:3, :] += jnp.sum(grad, axis=0, keepdims=True)
    sums_out[3:4, :] += jnp.sum(back, axis=0, keepdims=True)


def token_back_kernel(idx, tok, mid, mine, theirs, vec, out):
    grad = mine[...].astype(f32) + theirs[...].astype(f32)
    unit, inverse = norm_stats(tok[0].astype(f32))
    out[...] = (mid[...] + norm_back(unit, inverse, grad, vec[0:1, :])).astype(bf16)


def spread_kernel(nq, idx, *refs):
    pieces, out, flat = refs[:nq], refs[nq], refs[nq + 1]

    def some_columns(k, _):
        cols = pl.ds(pl.multiple_of(k * LANES, LANES), LANES)
        for j, piece in enumerate(pieces):
            images = piece.shape[0] // PAD
            for image in range(images):
                value = piece[image * PAD : (image + 1) * PAD, cols].astype(f32)
                flat[pl.ds((idx[j] * images + image) * SEQ, SEQ), :] = value[:SEQ]
        out[:, cols] = flat[...].astype(out.dtype)
        return 0

    lax.fori_loop(0, out.shape[1] // LANES, some_columns, 0)


def join_kernel(size, idx, *refs):
    pieces, out = refs[:size], refs[size]
    rows = pieces[0].shape[0]
    for j, piece in enumerate(pieces):
        out[pl.ds(pl.multiple_of(idx[j] * rows, rows), rows), :] = piece[...]


def weight_grad_kernel(idx, left_one, right_one, left_two, right_two, out):
    first = right_one.shape[1]
    out[:, :first] = dot_tn(left_one[...], right_one[...]).astype(bf16)
    out[:, first:] = dot_tn(left_two[...], right_two[...]).astype(bf16)


def split_grad_kernel(part, cut, idx, left_one, right_one, left_two, right_two, tail, *outs):
    i = pl.program_id(0)
    value = jnp.concatenate(
        [
            dot_tn(left_one[...], right_one[...]).astype(bf16),
            dot_tn(left_two[...], right_two[...]).astype(bf16),
            tail[...],
        ],
        axis=1,
    )
    blocks = value.shape[0] // part
    for block in range(blocks):
        at = pl.ds(pl.multiple_of((i * (blocks // 2) + block // 2) * part, part), part)
        rows = value[block * part : (block + 1) * part]
        for given in range(2):

            @pl.when((idx[0] == block % 2) != bool(given))
            def _():
                outs[given][at, :] = rows[:, :cut]
                outs[2 + given][at, :] = rows[:, cut:]


def adam_values(param, first, second, grad, decay):
    scaled = grad / loss_scale
    first = first_decay * first + (1.0 - first_decay) * scaled
    second = second_decay * second + (1.0 - second_decay) * scaled * scaled
    corrected = (
        first
        / (1.0 - first_decay**step_count)
        / (jnp.sqrt(second / (1.0 - second_decay**step_count)) + adam_eps)
    )
    return param - rate * (corrected + decay * param), first, second


def adam_kernel(idx, grad, turned_grad, param, moments, turned, turned_moments, *outs):
    for turn, (g, p, m) in enumerate(((grad, param, moments), (turned_grad, turned, turned_moments))):
        share_out, new_out, mom_out = outs[3 * turn : 3 * turn + 3]
        value = g[...].astype(f32)
        value = value.T if turn else value.reshape(p.shape)
        share_out[...] = value
        new, first, second = adam_values(p[...], m[0], m[1], value, weight_decay)
        new_out[...] = new
        mom_out[0] = first
        mom_out[1] = second


def call(kernel, grid, idx, in_specs, out_specs, out_shapes, args, aliases=None, scratch=(), us=5):
    return pl.pallas_call(
        kernel,
        grid_spec=pltpu.PrefetchScalarGridSpec(
            num_scalar_prefetch=1,
            grid=grid,
            in_specs=in_specs,
            out_specs=out_specs,
            scratch_shapes=list(scratch),
        ),
        out_shape=out_shapes,
        input_output_aliases=aliases or {},
        compiler_params=PARAMS,
        cost_estimate=pl.CostEstimate(flops=us * 10**9, bytes_accessed=us * 3 * 10**6, transcendentals=0),
    )(idx, *args)


def sds(shape, dtype):
    return jax.ShapeDtypeStruct(shape, dtype)


def far_sds(shape, dtype):
    return pltpu.HBM(shape, dtype)


def out_there(value):
    return pltpu.with_memory_space_constraint(value, pltpu.HBM)


def shared_args(buffers, n_args):
    specs = [pl.BlockSpec(memory_space=pl.ANY)] * len(buffers)
    aliases = {1 + n_args + j: j for j in range(len(buffers))}
    return specs, list(buffers), aliases


def attn_fwd(idx, tok, w, vec, bias, buffers):
    nq, (quarters, rows, d), width = idx.shape[0], tok.shape, bias.shape[1]
    specs, extra, aliases = shared_args(buffers, 4)
    out = call(
        functools.partial(attn_fwd_kernel, width, len(buffers)),
        (nq,),
        idx,
        [picked((rows, d)), whole(w.shape), whole(vec.shape), whole(bias.shape)] + specs,
        [picked((rows, d)), picked((rows, 3 * width)), picked((rows, width))] + [whole((rows, d))] * nq,
        [far_sds((quarters, rows, n), bf16) for n in (d, 3 * width, width)] + [sds((rows, d), bf16)] * nq,
        [out_there(tok), w, vec, bias] + extra,
        aliases,
        us=12,
    )
    return out[:3], out[3:]


def ffn(idx, pieces, cot, w, bias, buffers):
    nq, (quarters, rows, d), width = idx.shape[0], cot.shape, bias.shape[1]
    specs, extra, aliases = shared_args(buffers, nq + 3)
    out = call(
        functools.partial(ffn_kernel, nq, len(buffers)),
        (nq,),
        idx,
        [whole((rows, d))] * nq + [picked((rows, d)), whole(w.shape), whole(bias.shape)] + specs,
        [picked((rows, d)), picked((rows, width)), picked((rows, width)), whole((8, width))]
        + [whole((rows, d))] * (2 * nq),
        [far_sds((quarters, rows, n), bf16) for n in (d, width, width)]
        + [sds((8, width), f32)]
        + [sds((rows, d), bf16)] * (2 * nq),
        list(pieces) + [out_there(cot), w, bias] + extra,
        aliases,
        [pltpu.VMEM((rows, d), bf16)],
        us=16,
    )
    return out[:3], out[3][0], out[4 : 4 + nq], out[4 + nq :]


def attn_bwd(idx, pieces, tok, qkv, w, buffers):
    nq, (quarters, rows, d), width = idx.shape[0], tok.shape, qkv.shape[2] // 3
    specs, extra, aliases = shared_args(buffers, nq + 3)
    out = call(
        functools.partial(attn_bwd_kernel, nq, width, len(buffers)),
        (nq,),
        idx,
        [whole((rows, d))] * nq + [picked((rows, d)), picked((rows, 3 * width)), whole(w.shape)] + specs,
        [picked((rows, d)), picked((rows, 3 * width)), whole((8, 3 * width)), whole((8, d))]
        + [whole((rows, d))] * nq,
        [far_sds((quarters, rows, d), bf16), far_sds((quarters, rows, 3 * width), bf16)]
        + [sds((8, 3 * width), f32), sds((8, d), f32)]
        + [sds((rows, d), bf16)] * nq,
        list(pieces) + [out_there(tok), out_there(qkv), w] + extra,
        aliases,
        [pltpu.VMEM((rows, d), bf16), pltpu.VMEM((rows, width), bf16)],
        us=16,
    )
    return out[:2], out[2][0], out[3][:2], out[4:]


def rowwise(kernel, idx, args, kinds, outs):
    rows, d = outs[0].shape
    steps = rows // PAD
    specs = {
        "q": lambda v: pl.BlockSpec((1, PAD, d), lambda i, idx: (idx[0], i, 0)),
        "r": lambda v: pl.BlockSpec((PAD, d), lambda i, idx: (i, 0)),
        "w": lambda v: whole(v.shape),
    }
    return call(
        kernel,
        (steps,),
        idx,
        [specs[kind.lower()](v) for kind, v in zip(kinds, args)],
        [specs["w" if o.shape[0] == 8 else "r"](o) for o in outs],
        outs,
        [out_there(v) if kind in "qR" else v for kind, v in zip(kinds, args)],
        us=3,
    )


def weight_grads(idx, left_one, right_one, left_two, right_two, tail=None, part=None, cut=None):
    d = left_one.shape[2]
    flat = [out_there(v.reshape(-1, v.shape[2])) for v in (left_one, right_one, left_two, right_two)]
    first, second = flat[1].shape[1], flat[3].shape[1]
    step = 256
    n = flat[0].shape[0]
    column = pl.BlockSpec((n, step), lambda i, idx: (0, i))
    specs = [column, whole((n, first)), column, whole((n, second))]
    if tail is None:
        return call(
            weight_grad_kernel,
            (d // step,),
            idx,
            specs,
            pl.BlockSpec((step, first + second), lambda i, idx: (i, 0)),
            sds((d, first + second), bf16),
            flat,
            us=14,
        )
    shapes = [(d // 2, cut)] * 2 + [(d // 2, first + second + tail.shape[1] - cut)] * 2
    return call(
        functools.partial(split_grad_kernel, part, cut),
        (d // step,),
        idx,
        specs + [pl.BlockSpec((step, tail.shape[1]), lambda i, idx: (i, 0))],
        [whole(shape) for shape in shapes],
        [sds(shape, bf16) for shape in shapes],
        flat + [tail],
        us=10,
    )


def adam_pair(idx, grad, turned_grad, param, moments, turned, turned_moments):
    args = [grad, turned_grad, param, moments, turned, turned_moments]
    outs = [sds(v.shape, f32) for v in (param, param, moments, turned, turned, turned_moments)]
    return call(
        adam_kernel, (1,), idx, [whole(v.shape) for v in args], [whole(o.shape) for o in outs], outs, args, us=6
    )


def spread(idx, pieces, dtype):
    rows, d = pieces[0].shape
    total = len(pieces) * rows // PAD * SEQ
    step = d // 2
    return call(
        functools.partial(spread_kernel, len(pieces)),
        (d // step,),
        idx,
        [pl.BlockSpec((rows, step), lambda i, idx: (0, i))] * len(pieces),
        pl.BlockSpec((total, step), lambda i, idx: (0, i)),
        sds((total, d), dtype),
        list(pieces),
        scratch=[pltpu.VMEM((total, LANES), f32)],
        us=4,
    )


def swap(value, flip, size):
    return lax.ppermute(value, TENSOR, [(k, k ^ flip) for k in range(size)])


def add_low(left, right):
    return (left.astype(f32) + right.astype(f32)).astype(bf16)


def tie(value, *after):
    return lax.optimization_barrier((value,) + after)[0]


def shard_swap(value, flip, size):
    return lax.ppermute(value, SHARD, [(k, k ^ flip) for k in range(size)])


def gather_shards(value, size):
    outer = [value] + [shard_swap(value, 2 * k, size) for k in range(1, size // 2)]
    pieces = []
    for piece in outer:
        pieces += [piece, shard_swap(piece, 1, size)]
    rows, columns = value.shape
    index = jnp.arange(size, dtype=jnp.int32) ^ lax.axis_index(SHARD).astype(jnp.int32)
    return call(
        functools.partial(join_kernel, size),
        (1,),
        index,
        [whole(value.shape)] * size,
        whole((size * rows, columns)),
        sds((size * rows, columns), value.dtype),
        pieces,
        us=3,
    ), outer[1]


def scatter_outer(kept, given, size):
    me = lax.axis_index(SHARD) // 2
    take = lambda array, at: lax.dynamic_index_in_dim(array, at, 0, keepdims=False)
    value = add_low(kept, given).reshape(size // 2, -1, kept.shape[1])
    return value, [take(value, me)] + [shard_swap(take(value, me ^ k), 2 * k, size) for k in range(1, size // 2)]


def add_all(values):
    return functools.reduce(jnp.add, [value.astype(f32) for value in values])


def adamw(param, moments, grad, decay):
    scaled = grad / loss_scale
    first = first_decay * moments[0] + (1.0 - first_decay) * scaled
    second = second_decay * moments[1] + (1.0 - second_decay) * scaled * scaled
    corrected = (
        first
        / (1.0 - first_decay**step_count)
        / (jnp.sqrt(second / (1.0 - second_decay**step_count)) + adam_eps)
    )
    return (param - rate * (corrected + decay * param), jnp.stack([first, second]))


def on_device(
    n_shard,
    n_tensor,
    tokens,
    cotangent,
    input_weight,
    input_moments,
    input_bias,
    input_bias_moments,
    output_weight,
    output_moments,
    expand_weight,
    expand_moments,
    expand_bias,
    expand_bias_moments,
    shrink_weight,
    shrink_moments,
    vectors,
    vector_moments,
):
    rows, d = tokens.shape
    images = rows // SEQ
    per = images // n_tensor
    part = d // n_shard
    width = input_weight.shape[2]
    hidden = expand_weight.shape[1]
    me = lax.axis_index(TENSOR).astype(jnp.int32)
    index = jnp.arange(n_tensor, dtype=jnp.int32) ^ me
    near, far, own = index[:2], index[2:], index[:1]

    small = jnp.concatenate([vectors, expand_bias.reshape(1, -1)], axis=0)
    small = jnp.pad(small, ((0, 0), (0, LANES - part)))
    bias_rows = jnp.pad(input_bias, ((0, 0), (0, LANES - input_bias.shape[1])))
    small = jnp.concatenate([small, bias_rows], axis=0)
    n_small = small.shape[0]
    small = jnp.pad(small, ((0, part - n_small), (0, 0)))
    pack_one = jnp.concatenate(
        [input_weight[c] for c in range(3)] + [output_weight.T, small], axis=1
    ).astype(bf16)
    pack_two = jnp.concatenate([expand_weight, shrink_weight.T], axis=1).astype(bf16)
    w_one, first = gather_shards(pack_one, n_shard)
    w_two = lax.all_gather(tie(pack_two, first), SHARD, axis=0, tiled=True)
    small = w_one[:, 4 * width :].reshape(n_shard, part, LANES)[:, :n_small].astype(f32)
    vec = jnp.pad(small[:, :6, :part].transpose(1, 0, 2).reshape(6, d), ((0, 2), (0, 0)))
    full_expand_bias = small[:, 6, :part].reshape(1, hidden)
    full_bias = small[:, 7:9, : width // n_shard].transpose(1, 0, 2).reshape(2, width)

    def padded(values):
        values = values.reshape(images, SEQ, d)
        values = jnp.pad(values, ((0, 0), (0, PAD - SEQ), (0, 0)))
        return values.reshape(n_tensor, per * PAD, d)

    tok, cot = padded(tokens), padded(cotangent)
    far = tie(far, cot)
    q_rows = per * PAD
    block = (q_rows, d)

    buffers, (p2, p3) = attn_fwd(far, tok, w_one, vec, full_bias, ())
    sum2 = add_low(p2, swap(p3, 1, n_tensor))
    cross = swap(sum2, 2, n_tensor)
    (inputs_all, qkv_all, ctx_all), (p0, p1) = attn_fwd(tie(near, sum2), tok, w_one, vec, full_bias, buffers)
    sum0 = add_low(p0, swap(p1, 1, n_tensor))
    attended, normed = rowwise(
        mid_kernel, own, [tok, sum0, cross, vec], "qrrw", [far_sds(block, f32), sds(block, bf16)]
    )

    def gather_rows(value):
        return (value, swap(value, 1, n_tensor)), swap(value, 2, n_tensor)

    def gather_far(over, *after):
        over = tie(over, *after)
        return over, swap(over, 1, n_tensor)

    near_x, over_x = gather_rows(normed)
    buffers, bias_near, shrink_near, mid_near = ffn(near, near_x, cot, w_two, full_expand_bias, ())
    far_x = gather_far(over_x, mid_near[0])
    ffn_all, bias_far, shrink_far, mid_far = ffn(far, far_x, cot, w_two, full_expand_bias, buffers)
    x_all, hid_all, pre_all = ffn_all

    def scatter_rows(near_parts, far_parts):
        over = add_low(far_parts[0], swap(far_parts[1], 1, n_tensor))
        return add_low(near_parts[0], swap(near_parts[1], 1, n_tensor)), over

    mid_mine, mid_over = scatter_rows(mid_near, mid_far)
    mid_theirs = swap(mid_over, 2, n_tensor)
    grads_two = weight_grads(tie(own, mid_over), x_all, pre_all, cot, hid_all)
    share_two = lax.psum_scatter(grads_two, SHARD, scatter_dimension=0, tiled=True)
    mid_theirs = tie(mid_theirs, grads_two)
    mid, mid_low, vec_mid = rowwise(
        mid_back_kernel,
        own,
        [attended, cot, mid_mine, mid_theirs, vec],
        "Rqrrw",
        [far_sds(block, f32), sds(block, bf16), sds((8, d), f32)],
    )

    near_m, over_m = gather_rows(mid_low)
    buffers, sums_near, vec_near, part_near = attn_bwd(near, near_m, tok, qkv_all, w_one, ())
    far_m = gather_far(over_m, part_near[0])
    shrink_mine, shrink_over = scatter_rows(shrink_near, shrink_far)
    shrink_theirs = swap(tie(shrink_over, part_near[0]), 2, n_tensor)
    (mid_all, grad_all), sums_far, vec_far, part_far = attn_bwd(far, far_m, tok, qkv_all, w_one, buffers)

    mine, over = scatter_rows(part_near, part_far)
    theirs = swap(over, 2, n_tensor)

    vec_grads = jnp.concatenate([vec_near + vec_far, vec_mid[:4], (bias_near + bias_far).reshape(1, d)])
    vec_grads = vec_grads.reshape(7, n_shard, part).transpose(1, 0, 2)
    vec_grads = jnp.pad(vec_grads, ((0, 0), (0, 0), (0, LANES - part)))
    sums = sums_near + sums_far
    bias_grads = jnp.stack([sums[:width], sums[2 * width :]]).reshape(2, n_shard, -1).transpose(1, 0, 2)
    bias_grads = jnp.pad(bias_grads, ((0, 0), (0, 0), (0, LANES - bias_grads.shape[2])))
    tail = jnp.concatenate([vec_grads, bias_grads], axis=1)
    tail = jnp.pad(tail, ((0, 0), (0, part - n_small), (0, 0))).reshape(d, LANES).astype(bf16)
    grads_one = weight_grads(
        tie(lax.axis_index(SHARD).astype(jnp.int32).reshape(1) % 2, over),
        inputs_all,
        grad_all,
        mid_all,
        ctx_all,
        tail,
        part,
        2 * width,
    )
    halves = [(kept, shard_swap(given, 1, n_shard)) for kept, given in (grads_one[:2], grads_one[2:])]

    theirs = tie(theirs, grads_one[0])
    (token_low,) = rowwise(token_back_kernel, own, [tok, mid, mine, theirs, vec], "qRrrw", [sds(block, bf16)])
    (kept_one, given_one), (kept_two, given_two) = halves
    half_one = scatter_outer(kept_one, tie(given_one, token_low), n_shard)
    halves = [half_one, scatter_outer(kept_two, tie(given_two, half_one[0]), n_shard)]
    result = attended + (shrink_mine.astype(f32) + shrink_theirs.astype(f32)) + vec[5]
    near_o, over_o = gather_rows(tie(result.astype(bf16), theirs))
    near_t, over_t = gather_rows(token_low)

    share_two = tie(share_two, *[half[0] for half in halves])
    share_expand, new_expand, mom_expand, share_shrink, new_shrink, mom_shrink = adam_pair(
        own, share_two[:, :hidden], share_two[:, hidden:], expand_weight, expand_moments, shrink_weight, shrink_moments
    )
    token_gradient = spread(index, near_t + gather_far(over_t, share_expand), f32)
    share_one, share_rest = [add_all([tie(half[1][0], token_gradient)] + half[1][1:]) for half in halves]
    small = share_rest[:n_small, 2 * width :]
    share_vectors = small[:6, :part]
    share_vectors = share_vectors + swap(share_vectors, 1, n_tensor)
    share_vectors = share_vectors + swap(share_vectors, 2, n_tensor)
    share_expand_bias = small[6, :part]
    share_bias = small[7:9, : width // n_shard]

    columns = jnp.concatenate([share_one, share_rest[:, :width]], axis=1)
    share_input, new_input, mom_input, share_output, new_output, mom_output = adam_pair(
        own,
        columns.reshape(part, 3, width).transpose(1, 0, 2),
        share_rest[:, width : 2 * width],
        input_weight,
        input_moments,
        output_weight,
        output_moments,
    )
    block_output = spread(index, near_o + gather_far(over_o, share_input), bf16)
    new_bias, mom_bias = adamw(input_bias, input_bias_moments, share_bias, 0.0)
    new_expand_bias, mom_expand_bias = adamw(
        expand_bias, expand_bias_moments, share_expand_bias, 0.0
    )
    new_vectors, mom_vectors = adamw(vectors, vector_moments, share_vectors, 0.0)
    return (
        block_output,
        token_gradient,
        share_input,
        share_bias,
        share_output,
        share_expand,
        share_expand_bias,
        share_shrink,
        share_vectors,
        new_input,
        new_bias,
        new_output,
        new_expand,
        new_expand_bias,
        new_shrink,
        new_vectors,
        mom_input,
        mom_bias,
        mom_output,
        mom_expand,
        mom_expand_bias,
        mom_shrink,
        mom_vectors,
    )


def solution(mesh):
    def body(*args):
        return on_device(mesh.shape[SHARD], mesh.shape[TENSOR], *args)

    return jax.shard_map(
        body,
        mesh=mesh,
        in_specs=(
            P(SHARD, None),
            P(SHARD, None),
            P(None, SHARD, TENSOR),
            P(None, None, SHARD, TENSOR),
            P(None, (TENSOR, SHARD)),
            P(None, None, (TENSOR, SHARD)),
            P(TENSOR, SHARD),
            P(None, TENSOR, SHARD),
            P(SHARD, TENSOR),
            P(None, SHARD, TENSOR),
            P((TENSOR, SHARD)),
            P(None, (TENSOR, SHARD)),
            P(TENSOR, SHARD),
            P(None, TENSOR, SHARD),
            P(None, SHARD),
            P(None, None, SHARD),
        ),
        out_specs=(
            P(SHARD, None),
            P(SHARD, None),
            P(None, SHARD, TENSOR),
            P(None, (TENSOR, SHARD)),
            P(TENSOR, SHARD),
            P(SHARD, TENSOR),
            P((TENSOR, SHARD)),
            P(TENSOR, SHARD),
            P(None, SHARD),
            P(None, SHARD, TENSOR),
            P(None, (TENSOR, SHARD)),
            P(TENSOR, SHARD),
            P(SHARD, TENSOR),
            P((TENSOR, SHARD)),
            P(TENSOR, SHARD),
            P(None, SHARD),
            P(None, None, SHARD, TENSOR),
            P(None, None, (TENSOR, SHARD)),
            P(None, TENSOR, SHARD),
            P(None, SHARD, TENSOR),
            P(None, (TENSOR, SHARD)),
            P(None, TENSOR, SHARD),
            P(None, None, SHARD),
        ),
        check_vma=False,
    )
```

profile of v0, /device:TPU:0, one launch (start us, length us, event | category | flops | bytes accessed | tf_op | source)
XLA Modules:
  0.0 355.1 jit_solution(4774671696890900288)
XLA Ops:
  11.5 3.1 collective-permute-start.1
  15.6 6.0 %collective-permute-done.1.refs_2_ = bf16[128,1152]{1,0:T(8,128)(2,1)S(1)} collective-permute-done((bf16[128,1152]{1,0:T(8,128)(2,1)S(1)}, bf16[128,1152]{1,0:T(8,128)(2,1)S(1)}, u32[]{:S(2)}, u32[]{:S(2)}) %collective-permute-start.1) | collective-permute-done | bytes 294944 | tf_op jit(solution)/shard_map/ppermute | solution.py:508
  21.7 3.8 %collective-permute-start.5 = (bf16[128,1152]{1,0:T(8,128)(2,1)S(1)}, bf16[128,1152]{1,0:T(8,128)(2,1)S(1)}, u32[]{:S(2)}, u32[]{:S(2)}) collective-permute-start(bf16[128,1152]{1,0:T(8,128)(2,1)S(1)} %pad_dynamic-update-slice_fusion.refs_0_), channel_id=1, source_target_pairs={{0,24},{4,28},{8,16},{12,20},{16,8},{20,12},{24,0},{28,4},{1,25},{... | collective-permute-start | bytes 884744 | tf_op jit(solution)/shard_map/ppermute | solution.py:508
  27.1 4.6 %reshape.146 = bf16[8,197,1024]{2,1,0:T(8,128)(2,1)} reshape(bf16[1576,1024]{1,0:T(8,128)(2,1)} %param.18) | data formatting | bytes 6455296 | tf_op jit(solution)/shard_map/reshape | solution.py:601
  31.6 4.8 %reshape.148 = bf16[8,197,1024]{2,1,0:T(8,128)(2,1)} reshape(bf16[1576,1024]{1,0:T(8,128)(2,1)} %param.19) | data formatting | bytes 6455296 | tf_op jit(solution)/shard_map/reshape | solution.py:601
  36.4 4.4 %pad.31 = bf16[8,208,1024]{2,1,0:T(8,128)(2,1)} pad(bf16[8,197,1024]{2,1,0:T(8,128)(2,1)} %reshape.146, bf16[]{:T(256)} %constant.106.clone.1), padding=0_0x0_11x0_0 | pad | bytes 6635522 | tf_op jit(solution)/shard_map/jit(_pad)/pad | solution.py:602
  45.7 20.9 %collective-permute-done.3.refs_4_ = bf16[128,1152]{1,0:T(8,128)(2,1)S(1)} collective-permute-done((bf16[128,1152]{1,0:T(8,128)(2,1)S(1)}, bf16[128,1152]{1,0:T(8,128)(2,1)S(1)}, u32[]{:S(2)}, u32[]{:S(2)}) %collective-permute-start.3) | collective-permute-done | bytes 294944 | tf_op jit(solution)/shard_map/ppermute | solution.py:508
  69.7 9.5 %collective-permute-done.4.refs_5_ = bf16[128,1152]{1,0:T(8,128)(2,1)S(1)} collective-permute-done((bf16[128,1152]{1,0:T(8,128)(2,1)S(1)}, bf16[128,1152]{1,0:T(8,128)(2,1)S(1)}, u32[]{:S(2)}, u32[]{:S(2)}) %collective-permute-start.4) | collective-permute-done | bytes 294944 | tf_op jit(solution)/shard_map/ppermute | solution.py:508
  83.9 11.2 %shard_map.336 = (bf16[4,416,1024]{2,1,0:T(8,128)(2,1)}, bf16[4,416,768]{2,1,0:T(8,128)(2,1)}, bf16[4,416,256]{2,1,0:T(8,128)(2,1)}, bf16[416,1024]{1,0:T(8,128)(2,1)S(1)}, bf16[416,1024]{1,0:T(8,128)(2,1)S(1)}) custom-call(s32[2]{0:T(128)S(1)} %get-tuple-element.100.idx, bf16[4,416,1024]{2,1,0:T(8,128)(2,1)} %bitcast.138, ...), custom_call_target="tpu_custom_call" | custom-call | flops 12000000000 | bytes 36000000 | tf_op jit(solution)/shard_map/pallas_call | solution.py:325
  97.8 10.7 %shard_map.337 = (bf16[4,416,1024]{2,1,0:T(8,128)(2,1)}, bf16[4,416,768]{2,1,0:T(8,128)(2,1)}, bf16[4,416,256]{2,1,0:T(8,128)(2,1)}, bf16[416,1024]{1,0:T(8,128)(2,1)S(1)}, bf16[416,1024]{1,0:T(8,128)(2,1)S(1)}) custom-call(s32[2]{0:T(128)S(1)} %get-tuple-element.103.idx, ...), custom_call_target="tpu_custom_call", output_to_operand_aliasing={{0}: (5, {}), {1}: (6, {}), {2}: (7, {})} | custom-call | flops 12000000000 | bytes 36000000 | tf_op jit(solution)/shard_map/pallas_call | solution.py:325
  111.3 18.7 %collective-permute-done.9.theirs = bf16[416,1024]{1,0:T(8,128)(2,1)S(1)} collective-permute-done((bf16[416,1024]{1,0:T(8,128)(2,1)S(1)}, bf16[416,1024]{1,0:T(8,128)(2,1)S(1)}, u32[]{:S(2)}, u32[]{:S(2)}) %collective-permute-start.9) | collective-permute-done | bytes 852000 | tf_op jit(solution)/shard_map/ppermute | solution.py:496
  129.9 2.8 shard_map.338
  139.6 13.6 %shard_map.339 = (bf16[4,416,1024]{2,1,0:T(8,128)(2,1)}, bf16[4,416,1024]{2,1,0:T(8,128)(2,1)}, bf16[4,416,1024]{2,1,0:T(8,128)(2,1)}, f32[8,1024]{1,0:T(8,128)S...) custom-call(s32[2]{0:T(128)S(1)} %get-tuple-element.103.idx, ...), custom_call_target="tpu_custom_call" | custom-call | flops 16000000000 | bytes 48000000 | tf_op jit(solution)/shard_map/pallas_call | solution.py:325
  157.9 12.9 %shard_map.340 = (bf16[4,416,1024]{2,1,0:T(8,128)(2,1)}, bf16[4,416,1024]{2,1,0:T(8,128)(2,1)}, bf16[4,416,1024]{2,1,0:T(8,128)(2,1)}, f32[8,1024]{1,0:T(8,128)S...) custom-call(s32[2]{0:T(128)S(1)} %get-tuple-element.100.idx, ...), custom_call_target="tpu_custom_call", output_to_operand_aliasing={{0}: (6, {}), {1}: (7, {}), {2}: (8, {})} | custom-call | flops 16000000000 | bytes 48000000 | tf_op jit(solution)/shard_map/pallas_call | solution.py:325
  175.7 12.0 %shard_map.341 = bf16[1024,2048]{1,0:T(8,128)(2,1)S(1)} custom-call(s32[1]{0:T(128)S(1)} %bitcast.133, bf16[1664,1024]{1,0:T(8,128)(2,1)} %bitcast.156, bf16[1664,1024]{1,0:T(8,128)(2,1)} %bitcast.158, bf16[1664,1024]{1,0:T(8,128)(2,1)} %bitcast.146, bf16[1664,1024]{1,0:T(8,128)(2,1)} %bitcast.157), custom_call_target="tpu_custom_call" | custom-call | flops 14000000000 | bytes 42000000 | tf_op jit(solution)/shard_map/pallas_call | solution.py:325
  191.3 4.5 %collective-permute-done.17.theirs = bf16[416,1024]{1,0:T(8,128)(2,1)} collective-permute-done((bf16[416,1024]{1,0:T(8,128)(2,1)}, bf16[416,1024]{1,0:T(8,128)(2,1)}, u32[]{:S(2)}, u32[]{:S(2)}) %collective-permute-start.17) | collective-permute-done | bytes 852000 | tf_op jit(solution)/shard_map/ppermute | solution.py:496
  195.7 4.2 %shard_map.342 = (f32[416,1024]{1,0:T(8,128)}, bf16[416,1024]{1,0:T(8,128)(2,1)S(1)}, f32[8,1024]{1,0:T(8,128)S(1)}) custom-call(s32[1]{0:T(128)S(1)} %bitcast.134, f32[416,1024]{1,0:T(8,128)} %get-tuple-element.109.attended, bf16[4,416,1024]{2,1,0:T(8,128)(2,1)} %bitcast.147, bf16[416,1024]{1,0:T(8,128)(2,1)S(1)} %add_convert_fusion.4.mine, ...), custom_call_target="tpu_custom_call" | custom-call | flops 3000000000 | bytes 9000000 | tf_op jit(solution)/shard_map/pallas_call | solution.py:325
  202.3 14.5 %shard_map.343 = (bf16[4,416,1024]{2,1,0:T(8,128)(2,1)}, bf16[4,416,768]{2,1,0:T(8,128)(2,1)}, f32[8,768]{1,0:T(8,128)S(1)}, f32[8,1024]{1,0:T(8,128)S(1)}, bf16...) custom-call(s32[2]{0:T(128)S(1)} %get-tuple-element.103.idx, bf16[416,1024]{1,0:T(8,128)(2,1)S(1)} %get-tuple-element.129.refs_0_, ...), custom_call_target="tpu_custom_call" | custom-call | flops 16000000000 | bytes 48000000 | tf_op jit(solution)/shard_map/pallas_call | solution.py:325
  216.8 4.6 %collective-permute-done.20.refs_0_ = bf16[416,1024]{1,0:T(8,128)(2,1)S(1)} collective-permute-done((bf16[416,1024]{1,0:T(8,128)(2,1)S(1)}, bf16[416,1024]{1,0:T(8,128)(2,1)S(1)}, u32[]{:S(2)}, u32[]{:S(2)}) %collective-permute-start.20) | collective-permute-done | bytes 852000 | tf_op jit(solution)/shard_map/ppermute | solution.py:496
  224.5 14.8 %shard_map.344 = (bf16[4,416,1024]{2,1,0:T(8,128)(2,1)}, bf16[4,416,768]{2,1,0:T(8,128)(2,1)}, f32[8,768]{1,0:T(8,128)S(1)}, f32[8,1024]{1,0:T(8,128)S(1)}, bf16...) custom-call(s32[2]{0:T(128)S(1)} %get-tuple-element.100.idx, ...), custom_call_target="tpu_custom_call", output_to_operand_aliasing={{0}: (6, {}), {1}: (7, {})} | custom-call | flops 16000000000 | bytes 48000000 | tf_op jit(solution)/shard_map/pallas_call | solution.py:325
  244.4 7.6 %shard_map.345 = (bf16[512,512]{1,0:T(8,128)(2,1)S(1)}, bf16[512,512]{1,0:T(8,128)(2,1)S(1)}, bf16[512,640]{1,0:T(8,128)(2,1)S(1)}, bf16[512,640]{1,0:T(8,128)(2,1)S(1)}) custom-call(s32[1]{0:T(128)S(6)} %select_n.30.idx, bf16[1664,1024]{1,0:T(8,128)(2,1)} %bitcast.159, bf16[1664,768]{1,0:T(8,128)(2,1)} %bitcast.160, bf16[1664,1024]{1,0:T(8,128)(2,1)} %bitcast.155, ...), custom_call_target="tpu_custom_call" | custom-call | flops 10000000000 | bytes 30000000 | tf_op jit(solution)/shard_map/pallas_call | solution.py:325
  256.1 8.8 %collective-permute-done.23.theirs = bf16[416,1024]{1,0:T(8,128)(2,1)S(1)} collective-permute-done((bf16[416,1024]{1,0:T(8,128)(2,1)S(1)}, bf16[416,1024]{1,0:T(8,128)(2,1)S(1)}, u32[]{:S(2)}, u32[]{:S(2)}) %collective-permute-start.23) | collective-permute-done | bytes 852000 | tf_op jit(solution)/shard_map/ppermute | solution.py:496
  264.9 3.4 shard_map.346.refs_0_
  269.0 4.0 %collective-permute-done.26 = bf16[512,512]{1,0:T(8,128)(2,1)S(1)} collective-permute-done((bf16[512,512]{1,0:T(8,128)(2,1)S(1)}, bf16[512,512]{1,0:T(8,128)(2,1)S(1)}, u32[]{:S(2)}, u32[]{:S(2)}) %collective-permute-start.26) | collective-permute-done | bytes 524320 | tf_op jit(solution)/shard_map/ppermute | solution.py:508
  273.9 12.6 %collective-permute-done.30 = bf16[512,640]{1,0:T(8,128)(2,1)S(1)} collective-permute-done((bf16[512,640]{1,0:T(8,128)(2,1)S(1)}, bf16[512,640]{1,0:T(8,128)(2,1)S(1)}, u32[]{:S(2)}, u32[]{:S(2)}) %collective-permute-start.30) | collective-permute-done | bytes 655392 | tf_op jit(solution)/shard_map/ppermute | solution.py:508
  291.0 3.0 shard_map.347
  294.1 2.6 add_convert_fusion.2.refs_0_
  305.6 4.3 %collective-permute-start.35 = (bf16[128,640]{1,0:T(8,128)(2,1)S(1)}, bf16[128,640]{1,0:T(8,128)(2,1)S(1)}, u32[]{:S(2)}, u32[]{:S(2)}) collective-permute-start(bf16[128,640]{1,0:T(8,128)(2,1)S(1)} %get-tuple-element.234), channel_id=1, source_target_pairs={{0,8},{4,12},{8,0},{12,4},{16,24},{20,28},{24,16},{28,20},{1,9},{5... | collective-permute-start | bytes 491528 | tf_op jit(solution)/shard_map/ppermute | solution.py:508
  309.8 5.3 %shard_map.348 = f32[1576,1024]{1,0:T(8,128)} custom-call(s32[4]{0:T(128)S(1)} %iota_xor_fusion.1.idx, bf16[416,1024]{1,0:T(8,128)(2,1)} %shard_map.346.refs_0_, bf16[416,1024]{1,0:T(8,128)(2,1)} %collective-permute-done.28.refs_1_, bf16[416,1024]{1,0:T(8,128)(2,1)} %collective-permute-done.29.refs_2_, bf16[416,1024]{1,0:T(8,128)(2,1)S(1)} %collective-permute-done.31.refs_3_), custom_call_target="tpu_custom_call" | custom-call | flops 4000000000 | bytes 12000000 | tf_op jit(solution)/shard_map/pallas_call | solution.py:325
  315.1 4.8 %collective-permute-done.36 = bf16[128,640]{1,0:T(8,128)(2,1)S(1)} collective-permute-done((bf16[128,640]{1,0:T(8,128)(2,1)S(1)}, bf16[128,640]{1,0:T(8,128)(2,1)S(1)}, u32[]{:S(2)}, u32[]{:S(2)}) %collective-permute-start.36) | collective-permute-done | bytes 163872 | tf_op jit(solution)/shard_map/ppermute | solution.py:508
  322.6 9.5 %collective-permute-done.33 = bf16[128,512]{0,1:T(8,128)(2,1)} collective-permute-done((bf16[128,512]{0,1:T(8,128)(2,1)}, bf16[128,512]{0,1:T(8,128)(2,1)}, u32[]{:S(2)}, u32[]{:S(2)}) %collective-permute-start.33) | collective-permute-done | bytes 131104 | tf_op jit(solution)/shard_map/ppermute | solution.py:508
  344.3 3.8 %shard_map.350 = bf16[1576,1024]{1,0:T(8,128)(2,1)} custom-call(s32[4]{0:T(128)S(1)} %iota_xor_fusion.1.idx, bf16[416,1024]{1,0:T(8,128)(2,1)S(1)} %add_convert_fusion.2.refs_0_, bf16[416,1024]{1,0:T(8,128)(2,1)} %collective-permute-done.24.refs_1_, bf16[416,1024]{1,0:T(8,128)(2,1)S(1)} %collective-permute-done.25.refs_2_, ...), custom_call_target="tpu_custom_call" | custom-call | flops 4000000000 | bytes 12000000 | tf_op jit(solution)/shard_map/pallas_call | solution.py:325
  (226 shorter events, 89.1 us)
Async XLA Ops:
  7.2 129.0 %all-gather.2.cloned.1.call-start = ((), (), s32[]{:S(2)}) async-start(), calls=%async_computation.1 | async-start | bytes 4718592 | tf_op jit(solution)/shard_map/all_gather | solution.py:594
  11.5 10.1 %collective-permute-start.1 = (bf16[128,1152]{1,0:T(8,128)(2,1)S(1)}, bf16[128,1152]{1,0:T(8,128)(2,1)S(1)}, u32[]{:S(2)}, u32[]{:S(2)}) collective-permute-start(bf16[128,1152]{1,0:T(8,128)(2,1)S(1)} %pad_dynamic-update-slice_fusion.refs_0_), channel_id=1, source_target_pairs={{0,8},{4,12},{8,0},{12,4},{16,24},{20,28},{24,16},{28,20},{1,9},{5... | collective-permute-start | bytes 884744 | tf_op jit(solution)/shard_map/ppermute | solution.py:508
  21.6 265.8 %reduce-scatter.2.cloned.1.call-start = ((), (), s32[]{:S(2)}) async-start(), calls=%async_computation.2 | async-start | bytes 4718592 | tf_op jit(solution)/shard_map/reduce_scatter | solution.py:639
  21.7 21.8 %collective-permute-start.5 = (bf16[128,1152]{1,0:T(8,128)(2,1)S(1)}, bf16[128,1152]{1,0:T(8,128)(2,1)S(1)}, u32[]{:S(2)}, u32[]{:S(2)}) collective-permute-start(bf16[128,1152]{1,0:T(8,128)(2,1)S(1)} %pad_dynamic-update-slice_fusion.refs_0_), channel_id=1, source_target_pairs={{0,24},{4,28},{8,16},{12,20},{16,8},{20,12},{24,0},{28,4},{1,25},{... | collective-permute-start | bytes 884744 | tf_op jit(solution)/shard_map/ppermute | solution.py:508
  25.5 41.1 %collective-permute-start.3 = (bf16[128,1152]{1,0:T(8,128)(2,1)S(1)}, bf16[128,1152]{1,0:T(8,128)(2,1)S(1)}, u32[]{:S(2)}, u32[]{:S(2)}) collective-permute-start(bf16[128,1152]{1,0:T(8,128)(2,1)S(1)} %pad_dynamic-update-slice_fusion.refs_0_), channel_id=1, source_target_pairs={{0,16},{4,20},{8,24},{12,28},{16,0},{20,4},{24,8},{28,12},{1,17},{... | collective-permute-start | bytes 884744 | tf_op jit(solution)/shard_map/ppermute | solution.py:508
  25.5 43.4 %collective-permute-start = (bf16[128,1152]{1,0:T(8,128)(2,1)S(1)}, bf16[128,1152]{1,0:T(8,128)(2,1)S(1)}, u32[]{:S(2)}, u32[]{:S(2)}) collective-permute-start(bf16[128,1152]{1,0:T(8,128)(2,1)S(1)} %pad_dynamic-update-slice_fusion.refs_0_), channel_id=1, source_target_pairs={{0,4},{4,0},{8,12},{12,8},{16,20},{20,16},{24,28},{28,24},{1,5},{5... | collective-permute-start | bytes 884744 | tf_op jit(solution)/shard_map/ppermute | solution.py:508
  43.0 36.2 %collective-permute-start.2 = (bf16[128,1152]{1,0:T(8,128)(2,1)S(1)}, bf16[128,1152]{1,0:T(8,128)(2,1)S(1)}, u32[]{:S(2)}, u32[]{:S(2)}) collective-permute-start(bf16[128,1152]{1,0:T(8,128)(2,1)S(1)} %collective-permute-done.1.refs_2_), channel_id=1, source_target_pairs={{0,4},{4,0},{8,12},{12,8},{16,20},{20,16},{24,28},{28,24},{1,5},{5... | collective-permute-start | bytes 884744 | tf_op jit(solution)/shard_map/ppermute | solution.py:508
  43.5 26.1 %collective-permute-start.6 = (bf16[128,1152]{1,0:T(8,128)(2,1)S(1)}, bf16[128,1152]{1,0:T(8,128)(2,1)S(1)}, u32[]{:S(2)}, u32[]{:S(2)}) collective-permute-start(bf16[128,1152]{1,0:T(8,128)(2,1)S(1)} %collective-permute-done.5.refs_6_), channel_id=1, source_target_pairs={{0,4},{4,0},{8,12},{12,8},{16,20},{20,16},{24,28},{28,24},{1,5},{5... | collective-permute-start | bytes 884744 | tf_op jit(solution)/shard_map/ppermute | solution.py:508
  66.6 12.5 %collective-permute-start.4 = (bf16[128,1152]{1,0:T(8,128)(2,1)S(1)}, bf16[128,1152]{1,0:T(8,128)(2,1)S(1)}, u32[]{:S(2)}, u32[]{:S(2)}) collective-permute-start(bf16[128,1152]{1,0:T(8,128)(2,1)S(1)} %collective-permute-done.3.refs_4_), channel_id=1, source_target_pairs={{0,4},{4,0},{8,12},{12,8},{16,20},{20,16},{24,28},{28,24},{1,5},{5... | collective-permute-start | bytes 884744 | tf_op jit(solution)/shard_map/ppermute | solution.py:508
  108.7 21.2 %collective-permute-start.9 = (bf16[416,1024]{1,0:T(8,128)(2,1)S(1)}, bf16[416,1024]{1,0:T(8,128)(2,1)S(1)}, u32[]{:S(2)}, u32[]{:S(2)}) collective-permute-start(bf16[416,1024]{1,0:T(8,128)(2,1)S(1)} %add_convert_fusion.8), channel_id=1, source_target_pairs={{0,2},{1,3},{2,0},{3,1},{4,6},{5,7},{6,4},{7,5},{8,10},{9,11},{10,... | collective-permute-start | bytes 2555912 | tf_op jit(solution)/shard_map/ppermute | solution.py:496
  132.7 21.6 %collective-permute-start.12 = (bf16[416,1024]{1,0:T(8,128)(2,1)}, bf16[416,1024]{1,0:T(8,128)(2,1)S(1)}, u32[]{:S(2)}, u32[]{:S(2)}) collective-permute-start(bf16[416,1024]{1,0:T(8,128)(2,1)} %get-tuple-element.110.refs_0_), channel_id=1, source_target_pairs={{0,2},{1,3},{2,0},{3,1},{4,6},{5,7},{6,4},{7,5},{8,10},{9,11},{10,... | collective-permute-start | bytes 2555912 | tf_op jit(solution)/shard_map/ppermute | solution.py:496
  170.9 18.8 %collective-permute-start.15 = (bf16[416,1024]{1,0:T(8,128)(2,1)}, bf16[416,1024]{1,0:T(8,128)(2,1)}, u32[]{:S(2)}, u32[]{:S(2)}) collective-permute-start(bf16[416,1024]{1,0:T(8,128)(2,1)} %get-tuple-element.121), channel_id=1, source_target_pairs={{0,1},{1,0},{2,3},{3,2},{4,5},{5,4},{6,7},{7,6},{8,9},{9,8},{10,11... | collective-permute-start | bytes 2555912 | tf_op jit(solution)/shard_map/ppermute | solution.py:496
  174.4 21.3 %collective-permute-start.17 = (bf16[416,1024]{1,0:T(8,128)(2,1)}, bf16[416,1024]{1,0:T(8,128)(2,1)}, u32[]{:S(2)}, u32[]{:S(2)}) collective-permute-start(bf16[416,1024]{1,0:T(8,128)(2,1)} %add_convert_fusion.3), channel_id=1, source_target_pairs={{0,2},{1,3},{2,0},{3,1},{4,6},{5,7},{6,4},{7,5},{8,10},{9,11},{10,... | collective-permute-start | bytes 2555912 | tf_op jit(solution)/shard_map/ppermute | solution.py:496
  199.9 21.9 %collective-permute-start.14 = (bf16[416,1024]{1,0:T(8,128)(2,1)S(1)}, bf16[416,1024]{1,0:T(8,128)(2,1)S(1)}, u32[]{:S(2)}, u32[]{:S(2)}) collective-permute-start(bf16[416,1024]{1,0:T(8,128)(2,1)S(1)} %copy-done.12), channel_id=1, source_target_pairs={{0,1},{1,0},{2,3},{3,2},{4,5},{5,4},{6,7},{7,6},{8,9},{9,8},{10,11... | collective-permute-start | bytes 2555912 | tf_op jit(solution)/shard_map/ppermute | solution.py:496
  200.4 20.9 %collective-permute-start.20 = (bf16[416,1024]{1,0:T(8,128)(2,1)S(1)}, bf16[416,1024]{1,0:T(8,128)(2,1)S(1)}, u32[]{:S(2)}, u32[]{:S(2)}) collective-permute-start(bf16[416,1024]{1,0:T(8,128)(2,1)S(1)} %get-tuple-element.129.refs_0_), channel_id=1, source_target_pairs={{0,2},{1,3},{2,0},{3,1},{4,6},{5,7},{6,4},{7,5},{8,10},{9,11},{10,... | collective-permute-start | bytes 2555912 | tf_op jit(solution)/shard_map/ppermute | solution.py:496
  221.4 72.7 %collective-permute-start.11 = (bf16[416,1024]{1,0:T(8,128)(2,1)}, bf16[416,1024]{1,0:T(8,128)(2,1)}, u32[]{:S(2)}, u32[]{:S(2)}) collective-permute-start(bf16[416,1024]{1,0:T(8,128)(2,1)} %get-tuple-element.113), channel_id=1, source_target_pairs={{0,1},{1,0},{2,3},{3,2},{4,5},{5,4},{6,7},{7,6},{8,9},{9,8},{10,11... | collective-permute-start | bytes 2555912 | tf_op jit(solution)/shard_map/ppermute | solution.py:496
  223.1 71.0 %collective-permute-start.19 = (bf16[416,1024]{1,0:T(8,128)(2,1)}, bf16[416,1024]{1,0:T(8,128)(2,1)}, u32[]{:S(2)}, u32[]{:S(2)}) collective-permute-start(bf16[416,1024]{1,0:T(8,128)(2,1)} %add_convert_fusion.5), channel_id=1, source_target_pairs={{0,2},{1,3},{2,0},{3,1},{4,6},{5,7},{6,4},{7,5},{8,10},{9,11},{10,... | collective-permute-start | bytes 2555912 | tf_op jit(solution)/shard_map/ppermute | solution.py:496
  224.5 30.1 %collective-permute-start.27 = (bf16[416,1024]{1,0:T(8,128)(2,1)}, bf16[416,1024]{1,0:T(8,128)(2,1)}, u32[]{:S(2)}, u32[]{:S(2)}) collective-permute-start(bf16[416,1024]{1,0:T(8,128)(2,1)} %get-tuple-element.155), channel_id=1, source_target_pairs={{0,1},{1,0},{2,3},{3,2},{4,5},{5,4},{6,7},{7,6},{8,9},{9,8},{10,11... | collective-permute-start | bytes 2555912 | tf_op jit(solution)/shard_map/ppermute | solution.py:496
  243.6 21.3 %collective-permute-start.23 = (bf16[416,1024]{1,0:T(8,128)(2,1)S(1)}, bf16[416,1024]{1,0:T(8,128)(2,1)S(1)}, u32[]{:S(2)}, u32[]{:S(2)}) collective-permute-start(bf16[416,1024]{1,0:T(8,128)(2,1)S(1)} %add_convert_fusion.1), channel_id=1, source_target_pairs={{0,2},{1,3},{2,0},{3,1},{4,6},{5,7},{6,4},{7,5},{8,10},{9,11},{10,... | collective-permute-start | bytes 2555912 | tf_op jit(solution)/shard_map/ppermute | solution.py:496
  252.0 20.9 %collective-permute-start.26 = (bf16[512,512]{1,0:T(8,128)(2,1)S(1)}, bf16[512,512]{1,0:T(8,128)(2,1)S(1)}, u32[]{:S(2)}, u32[]{:S(2)}) collective-permute-start(bf16[512,512]{1,0:T(8,128)(2,1)S(1)} %get-tuple-element.153), channel_id=1, source_target_pairs={{0,4},{4,0},{8,12},{12,8},{16,20},{20,16},{24,28},{28,24},{1,5},{5... | collective-permute-start | bytes 1572872 | tf_op jit(solution)/shard_map/ppermute | solution.py:508
  254.6 31.9 %collective-permute-start.30 = (bf16[512,640]{1,0:T(8,128)(2,1)S(1)}, bf16[512,640]{1,0:T(8,128)(2,1)S(1)}, u32[]{:S(2)}, u32[]{:S(2)}) collective-permute-start(bf16[512,640]{1,0:T(8,128)(2,1)S(1)} %get-tuple-element.158), channel_id=1, source_target_pairs={{0,4},{4,0},{8,12},{12,8},{16,20},{20,16},{24,28},{28,24},{1,5},{5... | collective-permute-start | bytes 1966088 | tf_op jit(solution)/shard_map/ppermute | solution.py:508
  268.3 25.7 %collective-permute-start.29 = (bf16[416,1024]{1,0:T(8,128)(2,1)}, bf16[416,1024]{1,0:T(8,128)(2,1)}, u32[]{:S(2)}, u32[]{:S(2)}) collective-permute-start(bf16[416,1024]{1,0:T(8,128)(2,1)} %shard_map.346.refs_0_), channel_id=1, source_target_pairs={{0,2},{1,3},{2,0},{3,1},{4,6},{5,7},{6,4},{7,5},{8,10},{9,11},{10,... | collective-permute-start | bytes 2555912 | tf_op jit(solution)/shard_map/ppermute | solution.py:496
  273.0 32.5 %collective-permute-start.28 = (bf16[416,1024]{1,0:T(8,128)(2,1)}, bf16[416,1024]{1,0:T(8,128)(2,1)}, u32[]{:S(2)}, u32[]{:S(2)}) collective-permute-start(bf16[416,1024]{1,0:T(8,128)(2,1)} %shard_map.346.refs_0_), channel_id=1, source_target_pairs={{0,1},{1,0},{2,3},{3,2},{4,5},{5,4},{6,7},{7,6},{8,9},{9,8},{10,11... | collective-permute-start | bytes 2555912 | tf_op jit(solution)/shard_map/ppermute | solution.py:496
  294.0 11.5 %collective-permute-start.31 = (bf16[416,1024]{1,0:T(8,128)(2,1)}, bf16[416,1024]{1,0:T(8,128)(2,1)S(1)}, u32[]{:S(2)}, u32[]{:S(2)}) collective-permute-start(bf16[416,1024]{1,0:T(8,128)(2,1)} %collective-permute-done.29.refs_2_), channel_id=1, source_target_pairs={{0,1},{1,0},{2,3},{3,2},{4,5},{5,4},{6,7},{7,6},{8,9},{9,8},{10,11... | collective-permute-start | bytes 2555912 | tf_op jit(solution)/shard_map/ppermute | solution.py:496
  296.7 42.1 %collective-permute-start.25 = (bf16[416,1024]{1,0:T(8,128)(2,1)S(1)}, bf16[416,1024]{1,0:T(8,128)(2,1)S(1)}, u32[]{:S(2)}, u32[]{:S(2)}) collective-permute-start(bf16[416,1024]{1,0:T(8,128)(2,1)S(1)} %add_convert_fusion.2.refs_0_), channel_id=1, source_target_pairs={{0,2},{1,3},{2,0},{3,1},{4,6},{5,7},{6,4},{7,5},{8,10},{9,11},{10,... | collective-permute-start | bytes 2555912 | tf_op jit(solution)/shard_map/ppermute | solution.py:496
  298.1 46.3 %collective-permute-start.24 = (bf16[416,1024]{1,0:T(8,128)(2,1)S(1)}, bf16[416,1024]{1,0:T(8,128)(2,1)}, u32[]{:S(2)}, u32[]{:S(2)}) collective-permute-start(bf16[416,1024]{1,0:T(8,128)(2,1)S(1)} %add_convert_fusion.2.refs_0_), channel_id=1, source_target_pairs={{0,1},{1,0},{2,3},{3,2},{4,5},{5,4},{6,7},{7,6},{8,9},{9,8},{10,11... | collective-permute-start | bytes 2555912 | tf_op jit(solution)/shard_map/ppermute | solution.py:496
  305.4 9.7 %collective-permute-start.37 = (bf16[128,640]{1,0:T(8,128)(2,1)S(1)}, bf16[128,640]{1,0:T(8,128)(2,1)S(1)}, u32[]{:S(2)}, u32[]{:S(2)}) collective-permute-start(bf16[128,640]{1,0:T(8,128)(2,1)S(1)} %get-tuple-element.232), channel_id=1, source_target_pairs={{0,24},{4,28},{8,16},{12,20},{16,8},{20,12},{24,0},{28,4},{1,25},{... | collective-permute-start | bytes 491528 | tf_op jit(solution)/shard_map/ppermute | solution.py:508
  305.4 14.5 %collective-permute-start.36 = (bf16[128,640]{1,0:T(8,128)(2,1)S(1)}, bf16[128,640]{1,0:T(8,128)(2,1)S(1)}, u32[]{:S(2)}, u32[]{:S(2)}) collective-permute-start(bf16[128,640]{1,0:T(8,128)(2,1)S(1)} %get-tuple-element.233), channel_id=1, source_target_pairs={{0,16},{4,20},{8,24},{12,28},{16,0},{20,4},{24,8},{28,12},{1,17},{... | collective-permute-start | bytes 491528 | tf_op jit(solution)/shard_map/ppermute | solution.py:508
  305.6 14.4 %collective-permute-start.35 = (bf16[128,640]{1,0:T(8,128)(2,1)S(1)}, bf16[128,640]{1,0:T(8,128)(2,1)S(1)}, u32[]{:S(2)}, u32[]{:S(2)}) collective-permute-start(bf16[128,640]{1,0:T(8,128)(2,1)S(1)} %get-tuple-element.234), channel_id=1, source_target_pairs={{0,8},{4,12},{8,0},{12,4},{16,24},{20,28},{24,16},{28,20},{1,9},{5... | collective-permute-start | bytes 491528 | tf_op jit(solution)/shard_map/ppermute | solution.py:508
  320.0 12.2 %collective-permute-start.33 = (bf16[128,512]{0,1:T(8,128)(2,1)}, bf16[128,512]{0,1:T(8,128)(2,1)}, u32[]{:S(2)}, u32[]{:S(2)}) collective-permute-start(bf16[128,512]{0,1:T(8,128)(2,1)} %bitcast.32), channel_id=1, source_target_pairs={{0,16},{4,20},{8,24},{12,28},{16,0},{20,4},{24,8},{28,12},{1,17},{... | collective-permute-start | bytes 393224 | tf_op jit(solution)/shard_map/ppermute | solution.py:508
  320.0 12.2 %collective-permute-start.34 = (bf16[128,512]{0,1:T(8,128)(2,1)}, bf16[128,512]{0,1:T(8,128)(2,1)}, u32[]{:S(2)}, u32[]{:S(2)}) collective-permute-start(bf16[128,512]{0,1:T(8,128)(2,1)} %bitcast.33), channel_id=1, source_target_pairs={{0,24},{4,28},{8,16},{12,20},{16,8},{20,12},{24,0},{28,4},{1,25},{... | collective-permute-start | bytes 393224 | tf_op jit(solution)/shard_map/ppermute | solution.py:508
  322.6 16.8 %collective-permute-start.39 = (f32[6,128]{1,0:T(8,128)S(1)}, f32[6,128]{1,0:T(8,128)S(1)}, u32[]{:S(2)}, u32[]{:S(2)}) collective-permute-start(f32[6,128]{1,0:T(8,128)S(1)} %slice.176), channel_id=1, source_target_pairs={{0,1},{1,0},{2,3},{3,2},{4,5},{5,4},{6,7},{7,6},{8,9},{9,8},{10,11... | collective-permute-start | bytes 9224 | tf_op jit(solution)/shard_map/ppermute | solution.py:496
  (49 other events, 281.2 us)
Sparse Core Ops, SparseCore 0:
  21.8 87.4 all-gather.1
  189.9 91.2 reduce-scatter.1
where the time goes:
time: 360 us; the launch traced here: 355 us
  Pallas kernels  122 us (34%)
  waiting for transfers between devices  118 us (33%)
  local copies, waits for them, and re-layouts  45.5 us (13%)
  starting transfers between devices  32.9 us (9%)
  other arithmetic  21 us (6%)
  between operations  15 us (4%)
    pallas_call x16, Pallas kernels, call(): pl.pallas_call(kernel, grid_spec=pltpu.PrefetchScalarGridSpec(num_scalar_...  122 us
    ppermute x15, waiting for transfers between devices, shard_swap(): return lax.ppermute(value, SHARD, [(k, k ^ flip) for k in range(size)])  68 us
    ppermute x26, waiting for transfers between devices, swap(): return lax.ppermute(value, TENSOR, [(k, k ^ flip) for k in range(size)])  50.4 us
    ppermute x15, starting transfers between devices, shard_swap(): return lax.ppermute(value, SHARD, [(k, k ^ flip) for k in range(size)])  20.2 us
    unnamed x84, local copies, waits for them, and re-layouts  19.7 us
    ppermute x26, starting transfers between devices, swap(): return lax.ppermute(value, TENSOR, [(k, k ^ flip) for k in range(size)])  12.6 us
    convert_element_type x9, other arithmetic, add_low(): return (left.astype(f32) + right.astype(f32)).astype(bf16)  9.46 us
    reshape x2, local copies, waits for them, and re-layouts, padded(): values = values.reshape(images, SEQ, d)  9.33 us
  transfers between devices with their start and end apart: 43, of which 21 were waited for; matrix products, arithmetic and copies ran while one was open for 12% of the time, Pallas kernels for 30%

commit v1 on v0

--- a/solution.py
+++ b/solution.py
@@ -153,8 +153,20 @@
         return 0
 
     lax.fori_loop(0, width // step, some_columns, 0)
-    store_one(shrink_parts, i, dot_nt(hid_out[0], w[:, width:]).astype(bf16))
-    store_one(mid_parts, i, dot_nt(pre_out[0], w[:, :width]).astype(bf16))
+
+    def some_outputs(k, _):
+        at = pl.ds(pl.multiple_of(k * step, step), step)
+        for ref, value, start in ((shrink_parts, hid_out, width), (mid_parts, pre_out, 0)):
+            part = dot_nt(value[0], w[at, start : start + width]).astype(bf16)
+            for j in range(nq):
+
+                @pl.when(i == j)
+                def _():
+                    ref[j][:, at] = part
+
+        return 0
+
+    lax.fori_loop(0, x.shape[1] // step, some_outputs, 0)
 
 
 def attn_bwd_kernel(nq, width, shared, idx, *refs):
@@ -172,34 +184,36 @@
 
     ctx_grads[...] = ctx_grad
 
-    def one_image(image, _):
-        rows = pl.ds(pl.multiple_of(image * PAD, PAD), PAD)
-        for pair in range(width // LANES):
-            at = [slice(c * width + pair * LANES, c * width + (pair + 1) * LANES) for c in range(3)]
-            q2, k2, v2 = qkv[0, rows, at[0]] * scale, qkv[0, rows, at[1]], qkv[0, rows, at[2]]
-            c2 = ctx_grads[rows, pair * LANES : (pair + 1) * LANES]
-            outs = []
-            for half in range(LANES // HEAD):
-                mine = (lane // HEAD) == half
-                scores = dot_nt(k2, jnp.where(mine, q2, bf16(0)))
-                scores = jnp.where(live, scores, -1e30)
-                raised = jnp.exp(scores - jnp.max(scores, axis=0, keepdims=True))
-                prob = raised * (1.0 / jnp.sum(raised, axis=0, keepdims=True))
-                prob_grad = dot_nt(v2, jnp.where(mine, c2, bf16(0)))
-                row_dot = jnp.sum(prob_grad * prob, axis=0, keepdims=True)
-                score_grad = (prob * (prob_grad - row_dot)).astype(bf16)
-                outs.append(
-                    (
-                        dot_tn(score_grad, k2) * HEAD ** (-0.5),
-                        dot(score_grad, q2),
-                        dot(prob.astype(bf16), c2),
-                    )
+    pairs = width // LANES
+
+    def one_pair(step, _):
+        rows = pl.ds(pl.multiple_of(step // pairs * PAD, PAD), PAD)
+        start = step % pairs * LANES
+        at = [pl.ds(pl.multiple_of(c * width + start, LANES), LANES) for c in range(3)]
+        q2, k2, v2 = qkv[0, rows, at[0]] * scale, qkv[0, rows, at[1]], qkv[0, rows, at[2]]
+        c2 = ctx_grads[rows, at[0]]
+        outs = []
+        for half in range(LANES // HEAD):
+            mine = (lane // HEAD) == half
+            scores = dot_nt(k2, jnp.where(mine, q2, bf16(0)))
+            scores = jnp.where(live, scores, -1e30)
+            raised = jnp.exp(scores - jnp.max(scores, axis=0, keepdims=True))
+            prob = raised * (1.0 / jnp.sum(raised, axis=0, keepdims=True))
+            prob_grad = dot_nt(v2, jnp.where(mine, c2, bf16(0)))
+            row_dot = jnp.sum(prob_grad * prob, axis=0, keepdims=True)
+            score_grad = (prob * (prob_grad - row_dot)).astype(bf16)
+            outs.append(
+                (
+                    dot_tn(score_grad, k2) * HEAD ** (-0.5),
+                    dot(score_grad, q2),
+                    dot(prob.astype(bf16), c2),
                 )
-            for c in range(3):
-                grad_out[0, rows, at[c]] = jnp.where(lane < HEAD, outs[0][c], outs[1][c]).astype(bf16)
+            )
+        for c in range(3):
+            grad_out[0, rows, at[c]] = jnp.where(lane < HEAD, outs[0][c], outs[1][c]).astype(bf16)
         return 0
 
-    lax.fori_loop(0, tok.shape[1] // PAD, one_image, 0)
+    lax.fori_loop(0, tok.shape[1] // PAD * pairs, one_pair, 0)
     grads = grad_out[0]
     part = dot_nt(grads, w[:, : 3 * width])
     store_one(parts, i, part.astype(bf16))
@@ -309,16 +323,61 @@
     return param - rate * (corrected + decay * param), first, second
 
 
-def adam_kernel(idx, grad, turned_grad, param, moments, turned, turned_moments, *outs):
-    for turn, (g, p, m) in enumerate(((grad, param, moments), (turned_grad, turned, turned_moments))):
-        share_out, new_out, mom_out = outs[3 * turn : 3 * turn + 3]
-        value = g[...].astype(f32)
-        value = value.T if turn else value.reshape(p.shape)
-        share_out[...] = value
-        new, first, second = adam_values(p[...], m[0], m[1], value, weight_decay)
-        new_out[...] = new
-        mom_out[0] = first
-        mom_out[1] = second
+def adam_store(value, p, m, share_out, new_out, mom_out):
+    share_out[...] = value
+    new_out[...], mom_out[0], mom_out[1] = adam_values(p[...], m[0], m[1], value, weight_decay)
+
+
+def adam_hidden_kernel(idx, grad, turned_grad, param, moments, turned, turned_moments, *outs):
+    adam_store(grad[...].astype(f32), param, moments, *outs[:3])
+    adam_store(turned_grad[...].astype(f32).T, turned, turned_moments, *outs[3:])
+
+
+def adam_attention_kernel(n, idx, *refs):
+    first, second, (param, moments, turned, turned_moments), outs = refs[:n], refs[n : 2 * n], refs[2 * n : 2 * n + 4], refs[2 * n + 4 :]
+    one = functools.reduce(jnp.add, [ref[...].astype(f32) for ref in first])
+    two = functools.reduce(jnp.add, [ref[...].astype(f32) for ref in second])
+    width = param.shape[2]
+    for c, value in enumerate((one[:, :width], one[:, width:], two[:, :width])):
+        adam_store(value, param.at[c], moments.at[:, c], outs[0].at[c], outs[1].at[c], outs[2].at[:, c])
+    adam_store(two[:, width : 2 * width].T, turned, turned_moments, *outs[3:6])
+    outs[6][...] = two[:, 2 * width :]
+
+
+def sum_kernel(idx, kept, given, *outs):
+    rows = outs[0].shape[0]
+    for k, out in enumerate(outs):
+        at = pl.ds(pl.multiple_of((idx[0] ^ k) * rows, rows), rows)
+        out[...] = (kept[at, :].astype(f32) + given[at, :].astype(f32)).astype(bf16)
+
+
+def pad_kernel(idx, values, out, flat):
+    rows = values.shape[0]
+    live = lax.broadcasted_iota(jnp.int32, (PAD, 1), 0) < SEQ
+    per = out.shape[1] // PAD
+
+    def some_columns(k, _):
+        cols = pl.ds(pl.multiple_of(k * LANES, LANES), LANES)
+        flat[:rows, :] = values[:, cols].astype(f32)
+        for image in range(rows // SEQ):
+            value = jnp.where(live, flat[image * SEQ : image * SEQ + PAD, :], 0.0)
+            at = slice(image % per * PAD, (image % per + 1) * PAD)
+            out[image // per, at, cols] = value.astype(bf16)
+        return 0
+
+    lax.fori_loop(0, values.shape[1] // LANES, some_columns, 0)
+
+
+def pack_kernel(idx, inner, outer, vectors, hidden_bias, bias, out, small):
+    part, width = inner.shape[1:]
+    for c in range(3):
+        out[:, c * width : (c + 1) * width] = inner[c].astype(bf16)
+    out[:, 3 * width : 4 * width] = outer[...].T.astype(bf16)
+    small[...] = jnp.zeros_like(small)
+    small[0:6, :part] = vectors[...]
+    small[6:7, :part] = hidden_bias[...]
+    small[7:9, : bias.shape[1]] = bias[...]
+    out[:, 4 * width :] = small[...].astype(bf16)
 
 
 def call(kernel, grid, idx, in_specs, out_specs, out_shapes, args, aliases=None, scratch=(), us=5):
@@ -467,11 +526,76 @@
     )
 
 
-def adam_pair(idx, grad, turned_grad, param, moments, turned, turned_moments):
-    args = [grad, turned_grad, param, moments, turned, turned_moments]
+def adam_hidden(idx, grads, param, moments, turned, turned_moments):
+    part, hidden = param.shape
+    step = 256
+    count = hidden // step
+    wide = pl.BlockSpec((part, step), lambda i, idx: (0, i))
+    wide_two = pl.BlockSpec((2, part, step), lambda i, idx: (0, 0, i))
+    tall = pl.BlockSpec((step, part), lambda i, idx: (i, 0))
+    tall_two = pl.BlockSpec((2, step, part), lambda i, idx: (0, i, 0))
+    beside = pl.BlockSpec((part, step), lambda i, idx: (0, i + count))
     outs = [sds(v.shape, f32) for v in (param, param, moments, turned, turned, turned_moments)]
     return call(
-        adam_kernel, (1,), idx, [whole(v.shape) for v in args], [whole(o.shape) for o in outs], outs, args, us=6
+        adam_hidden_kernel,
+        (count,),
+        idx,
+        [wide, beside, wide, wide_two, tall, tall_two],
+        [wide, wide, wide_two, tall, tall, tall_two],
+        outs,
+        [grads, grads, param, moments, turned, turned_moments],
+        us=4,
+    )
+
+
+def adam_attention(idx, first, second, param, moments, turned, turned_moments):
+    args = list(first) + list(second) + [param, moments, turned, turned_moments]
+    outs = [sds(v.shape, f32) for v in (param, param, moments, turned, turned, turned_moments)]
+    outs.append(sds((first[0].shape[0], LANES), f32))
+    return call(
+        functools.partial(adam_attention_kernel, len(first)),
+        (1,),
+        idx,
+        [whole(v.shape) for v in args],
+        [whole(o.shape) for o in outs],
+        outs,
+        args,
+        us=3,
+    )
+
+
+def padded(idx, values, quarters):
+    rows, d = values.shape
+    images = rows // SEQ
+    shape = (quarters, images // quarters * PAD, d)
+    step = d // 2
+    return call(
+        pad_kernel,
+        (d // step,),
+        idx,
+        [pl.BlockSpec((rows, step), lambda i, idx: (0, i))],
+        pl.BlockSpec(shape[:2] + (step,), lambda i, idx: (0, 0, i)),
+        far_sds(shape, bf16),
+        [values],
+        scratch=[pltpu.VMEM(((images - 1) * SEQ + PAD + 5, LANES), f32)],
+        us=4,
+    )
+
+
+def pack(idx, inner, outer, vectors, hidden_bias, bias):
+    part, width = inner.shape[1:]
+    args = [inner, outer, vectors, hidden_bias.reshape(1, -1), bias]
+    shape = (part, 4 * width + LANES)
+    return call(
+        pack_kernel,
+        (1,),
+        idx,
+        [whole(v.shape) for v in args],
+        whole(shape),
+        sds(shape, bf16),
+        args,
+        scratch=[pltpu.VMEM((part, LANES), f32)],
+        us=2,
     )
 
 
@@ -522,20 +646,26 @@
         [whole(value.shape)] * size,
         whole((size * rows, columns)),
         sds((size * rows, columns), value.dtype),
-        pieces,
+        [out_there(piece) for piece in pieces],
         us=3,
     ), outer[1]
 
 
 def scatter_outer(kept, given, size):
-    me = lax.axis_index(SHARD) // 2
-    take = lambda array, at: lax.dynamic_index_in_dim(array, at, 0, keepdims=False)
-    value = add_low(kept, given).reshape(size // 2, -1, kept.shape[1])
-    return value, [take(value, me)] + [shard_swap(take(value, me ^ k), 2 * k, size) for k in range(1, size // 2)]
-
-
-def add_all(values):
-    return functools.reduce(jnp.add, [value.astype(f32) for value in values])
+    count = size // 2
+    me = (lax.axis_index(SHARD) // 2).astype(jnp.int32).reshape(1)
+    shape = (kept.shape[0] // count, kept.shape[1])
+    own, *others = call(
+        sum_kernel,
+        (1,),
+        me,
+        [whole(kept.shape)] * 2,
+        [whole(shape)] * count,
+        [sds(shape, bf16)] * count,
+        [kept, given],
+        us=2,
+    )
+    return [own] + [shard_swap(other, 2 * k + 2, size) for k, other in enumerate(others)]
 
 
 def adamw(param, moments, grad, decay):
@@ -580,15 +710,8 @@
     index = jnp.arange(n_tensor, dtype=jnp.int32) ^ me
     near, far, own = index[:2], index[2:], index[:1]
 
-    small = jnp.concatenate([vectors, expand_bias.reshape(1, -1)], axis=0)
-    small = jnp.pad(small, ((0, 0), (0, LANES - part)))
-    bias_rows = jnp.pad(input_bias, ((0, 0), (0, LANES - input_bias.shape[1])))
-    small = jnp.concatenate([small, bias_rows], axis=0)
-    n_small = small.shape[0]
-    small = jnp.pad(small, ((0, part - n_small), (0, 0)))
-    pack_one = jnp.concatenate(
-        [input_weight[c] for c in range(3)] + [output_weight.T, small], axis=1
-    ).astype(bf16)
+    n_small = vectors.shape[0] + 1 + input_bias.shape[0]
+    pack_one = pack(own, input_weight, output_weight, vectors, expand_bias, input_bias)
     pack_two = jnp.concatenate([expand_weight, shrink_weight.T], axis=1).astype(bf16)
     w_one, first = gather_shards(pack_one, n_shard)
     w_two = lax.all_gather(tie(pack_two, first), SHARD, axis=0, tiled=True)
@@ -597,12 +720,7 @@
     full_expand_bias = small[:, 6, :part].reshape(1, hidden)
     full_bias = small[:, 7:9, : width // n_shard].transpose(1, 0, 2).reshape(2, width)
 
-    def padded(values):
-        values = values.reshape(images, SEQ, d)
-        values = jnp.pad(values, ((0, 0), (0, PAD - SEQ), (0, 0)))
-        return values.reshape(n_tensor, per * PAD, d)
-
-    tok, cot = padded(tokens), padded(cotangent)
+    tok, cot = [padded(own, values, n_tensor) for values in (tokens, cotangent)]
     far = tie(far, cot)
     q_rows = per * PAD
     block = (q_rows, d)
@@ -679,36 +797,28 @@
     theirs = tie(theirs, grads_one[0])
     (token_low,) = rowwise(token_back_kernel, own, [tok, mid, mine, theirs, vec], "qRrrw", [sds(block, bf16)])
     (kept_one, given_one), (kept_two, given_two) = halves
-    half_one = scatter_outer(kept_one, tie(given_one, token_low), n_shard)
-    halves = [half_one, scatter_outer(kept_two, tie(given_two, half_one[0]), n_shard)]
+    halves = [scatter_outer(kept_one, tie(given_one, token_low), n_shard), scatter_outer(kept_two, given_two, n_shard)]
     result = attended + (shrink_mine.astype(f32) + shrink_theirs.astype(f32)) + vec[5]
     near_o, over_o = gather_rows(tie(result.astype(bf16), theirs))
     near_t, over_t = gather_rows(token_low)
 
-    share_two = tie(share_two, *[half[0] for half in halves])
-    share_expand, new_expand, mom_expand, share_shrink, new_shrink, mom_shrink = adam_pair(
-        own, share_two[:, :hidden], share_two[:, hidden:], expand_weight, expand_moments, shrink_weight, shrink_moments
+    share_two = tie(share_two, halves[1][0])
+    share_expand, new_expand, mom_expand, share_shrink, new_shrink, mom_shrink = adam_hidden(
+        own, share_two, expand_weight, expand_moments, shrink_weight, shrink_moments
     )
     token_gradient = spread(index, near_t + gather_far(over_t, share_expand), f32)
-    share_one, share_rest = [add_all([tie(half[1][0], token_gradient)] + half[1][1:]) for half in halves]
-    small = share_rest[:n_small, 2 * width :]
-    share_vectors = small[:6, :part]
-    share_vectors = share_vectors + swap(share_vectors, 1, n_tensor)
-    share_vectors = share_vectors + swap(share_vectors, 2, n_tensor)
+    block_output = spread(index, near_o + gather_far(over_o, token_gradient), bf16)
+    first, second = [[tie(half[0], block_output)] + half[1:] for half in halves]
+    share_input, new_input, mom_input, share_output, new_output, mom_output, small = adam_attention(
+        own, first, second, input_weight, input_moments, output_weight, output_moments
+    )
+    own_vectors = small[:6, :part]
+    share_vectors = functools.reduce(
+        jnp.add, [own_vectors] + [swap(own_vectors, k, n_tensor) for k in range(1, n_tensor)]
+    )
     share_expand_bias = small[6, :part]
     share_bias = small[7:9, : width // n_shard]
 
-    columns = jnp.concatenate([share_one, share_rest[:, :width]], axis=1)
-    share_input, new_input, mom_input, share_output, new_output, mom_output = adam_pair(
-        own,
-        columns.reshape(part, 3, width).transpose(1, 0, 2),
-        share_rest[:, width : 2 * width],
-        input_weight,
-        input_moments,
-        output_weight,
-        output_moments,
-    )
-    block_output = spread(index, near_o + gather_far(over_o, share_input), bf16)
     new_bias, mom_bias = adamw(input_bias, input_bias_moments, share_bias, 0.0)
     new_expand_bias, mom_expand_bias = adamw(
         expand_bias, expand_bias_moments, share_expand_bias, 0.0

time: 360 us -> 358 us (level); the launches traced: 355 us -> 357 us
  local copies, waits for them, and re-layouts: 45.5 us -> 25.9 us
  starting transfers between devices: 32.9 us -> 47.4 us
  Pallas kernels: 122 us -> 135 us
  other arithmetic: 21 us -> 14.6 us
    ppermute x15, waiting for transfers between devices: 68 us -> 41.3 us  [shard_swap(): return lax.ppermute(value, SHARD, [(k, k ^ flip) for k in range(size)])]
    ppermute x26 -> x27, waiting for transfers between devices: 50.4 us -> 74.9 us  [swap(): return lax.ppermute(value, TENSOR, [(k, k ^ flip) for k in range(size)])]
    pallas_call x16 -> x21, Pallas kernels: 122 us -> 135 us  [call(): pl.pallas_call(kernel, grid_spec=pltpu.PrefetchScalarGridSpec(num_scalar_...]
    ppermute x15, starting transfers between devices: 20.2 us -> 32.1 us  [shard_swap(): return lax.ppermute(value, SHARD, [(k, k ^ flip) for k in range(size)])]
    reshape x3 -> x0, local copies, waits for them, and re-layouts: 10.5 us -> none  [the longest x2 9.33 us: padded(): values = values.reshape(images, SEQ, d)]
    pad x2 -> x0, local copies, waits for them, and re-layouts: 6.56 us -> none  [padded(): values = jnp.pad(values, ((0, 0), (0, PAD - SEQ), (0, 0)))]
    dynamic_slice x5 -> x0, local copies, waits for them, and re-layouts: 5.86 us -> none  [scatter_outer(): lax.dynamic_index_in_dim(array, at, 0, keepdims=False)]
    unnamed x84 -> x109, local copies, waits for them, and re-layouts: 19.7 us -> 24.3 us
  transfers between devices with their start and end apart: 43 -> 44, of which waited for: 21 -> 26; matrix products, arithmetic and copies ran while one was open for 12% -> 4% of each run, Pallas kernels for 30% -> 33%
where the time goes in v1:
time: 358 us; the launch traced here: 357 us
  Pallas kernels  135 us (38%)
  waiting for transfers between devices  120 us (34%)
  starting transfers between devices  47.4 us (13%)
  local copies, waits for them, and re-layouts  25.9 us (7%)
  other arithmetic  14.6 us (4%)
  between operations  14.6 us (4%)
    pallas_call x21, Pallas kernels, call(): pl.pallas_call(kernel, grid_spec=pltpu.PrefetchScalarGridSpec(num_scalar_...  135 us
    ppermute x27, waiting for transfers between devices, swap(): return lax.ppermute(value, TENSOR, [(k, k ^ flip) for k in range(size)])  74.9 us
    ppermute x15, waiting for transfers between devices, shard_swap(): return lax.ppermute(value, SHARD, [(k, k ^ flip) for k in range(size)])  41.3 us
    ppermute x15, starting transfers between devices, shard_swap(): return lax.ppermute(value, SHARD, [(k, k ^ flip) for k in range(size)])  32.1 us
    unnamed x109, local copies, waits for them, and re-layouts  24.3 us
    ppermute x27, starting transfers between devices, swap(): return lax.ppermute(value, TENSOR, [(k, k ^ flip) for k in range(size)])  15.2 us
    convert_element_type x7, other arithmetic, add_low(): return (left.astype(f32) + right.astype(f32)).astype(bf16)  8.67 us
  transfers between devices with their start and end apart: 44, of which 26 were waited for; matrix products, arithmetic and copies ran while one was open for 4% of the time, Pallas kernels for 33%

profile of v1, /device:TPU:0, one launch (start us, length us, event | category | flops | bytes accessed | tf_op | source)
XLA Modules:
  0.0 357.3 jit_solution(15070890827502599108)
XLA Ops:
  11.3 3.1 collective-permute-start.1
  23.9 2.5 shard_map.336.refs_2_.cot
  28.0 3.2 collective-permute-done.5.refs_6_
  32.7 17.8 %collective-permute-done.3.refs_4_ = bf16[128,1152]{1,0:T(8,128)(2,1)S(1)} collective-permute-done((bf16[128,1152]{1,0:T(8,128)(2,1)S(1)}, bf16[128,1152]{1,0:T(8,128)(2,1)S(1)}, u32[]{:S(2)}, u32[]{:S(2)}) %collective-permute-start.3) | collective-permute-done | bytes 294944 | tf_op jit(solution)/shard_map/ppermute | solution.py:632
  54.4 2.6 shard_map.335.tok.refs_2_
  61.6 10.8 %shard_map.339 = (bf16[4,416,1024]{2,1,0:T(8,128)(2,1)}, bf16[4,416,768]{2,1,0:T(8,128)(2,1)}, bf16[4,416,256]{2,1,0:T(8,128)(2,1)}, bf16[416,1024]{1,0:T(8,128)(2,1)S(1)}, bf16[416,1024]{1,0:T(8,128)(2,1)S(1)}) custom-call(s32[2]{0:T(128)S(1)} %get-tuple-element.108.idx, bf16[4,416,1024]{2,1,0:T(8,128)(2,1)} %shard_map.335.tok.refs_2_, ...), custom_call_target="tpu_custom_call" | custom-call | flops 12000000000 | bytes 36000000 | tf_op jit(solution)/shard_map/pallas_call | solution.py:384
  75.1 10.8 %shard_map.340 = (bf16[4,416,1024]{2,1,0:T(8,128)(2,1)}, bf16[4,416,768]{2,1,0:T(8,128)(2,1)}, bf16[4,416,256]{2,1,0:T(8,128)(2,1)}, bf16[416,1024]{1,0:T(8,128)(2,1)S(1)}, bf16[416,1024]{1,0:T(8,128)(2,1)S(1)}) custom-call(s32[2]{0:T(128)S(1)} %get-tuple-element.111.idx, ...), custom_call_target="tpu_custom_call", output_to_operand_aliasing={{0}: (5, {}), {1}: (6, {}), {2}: (7, {})} | custom-call | flops 12000000000 | bytes 36000000 | tf_op jit(solution)/shard_map/pallas_call | solution.py:384
  88.6 18.7 %collective-permute-done.9.theirs = bf16[416,1024]{1,0:T(8,128)(2,1)S(1)} collective-permute-done((bf16[416,1024]{1,0:T(8,128)(2,1)S(1)}, bf16[416,1024]{1,0:T(8,128)(2,1)S(1)}, u32[]{:S(2)}, u32[]{:S(2)}) %collective-permute-start.9) | collective-permute-done | bytes 852000 | tf_op jit(solution)/shard_map/ppermute | solution.py:620
  107.2 2.8 shard_map.341
  116.9 14.4 %shard_map.342 = (bf16[4,416,1024]{2,1,0:T(8,128)(2,1)}, bf16[4,416,1024]{2,1,0:T(8,128)(2,1)}, bf16[4,416,1024]{2,1,0:T(8,128)(2,1)}, f32[8,1024]{1,0:T(8,128)S...) custom-call(s32[2]{0:T(128)S(1)} %get-tuple-element.111.idx, ...), custom_call_target="tpu_custom_call" | custom-call | flops 16000000000 | bytes 48000000 | tf_op jit(solution)/shard_map/pallas_call | solution.py:384
  135.2 14.1 %shard_map.343 = (bf16[4,416,1024]{2,1,0:T(8,128)(2,1)}, bf16[4,416,1024]{2,1,0:T(8,128)(2,1)}, bf16[4,416,1024]{2,1,0:T(8,128)(2,1)}, f32[8,1024]{1,0:T(8,128)S...) custom-call(s32[2]{0:T(128)S(1)} %get-tuple-element.108.idx, ...), custom_call_target="tpu_custom_call", output_to_operand_aliasing={{0}: (6, {}), {1}: (7, {}), {2}: (8, {})} | custom-call | flops 16000000000 | bytes 48000000 | tf_op jit(solution)/shard_map/pallas_call | solution.py:384
  154.4 12.1 %shard_map.344 = bf16[1024,2048]{1,0:T(8,128)(2,1)S(1)} custom-call(s32[1]{0:T(128)S(1)} %bitcast.103, bf16[1664,1024]{1,0:T(8,128)(2,1)} %bitcast.114, bf16[1664,1024]{1,0:T(8,128)(2,1)} %bitcast.116, bf16[1664,1024]{1,0:T(8,128)(2,1)} %bitcast.112, bf16[1664,1024]{1,0:T(8,128)(2,1)} %bitcast.115), custom_call_target="tpu_custom_call" | custom-call | flops 14000000000 | bytes 42000000 | tf_op jit(solution)/shard_map/pallas_call | solution.py:384
  170.0 4.2 %collective-permute-done.17.theirs = bf16[416,1024]{1,0:T(8,128)(2,1)} collective-permute-done((bf16[416,1024]{1,0:T(8,128)(2,1)}, bf16[416,1024]{1,0:T(8,128)(2,1)}, u32[]{:S(2)}, u32[]{:S(2)}) %collective-permute-start.17) | collective-permute-done | bytes 852000 | tf_op jit(solution)/shard_map/ppermute | solution.py:620
  174.2 4.2 %shard_map.345 = (f32[416,1024]{1,0:T(8,128)}, bf16[416,1024]{1,0:T(8,128)(2,1)S(1)}, f32[8,1024]{1,0:T(8,128)S(1)}) custom-call(s32[1]{0:T(128)S(1)} %bitcast.104, f32[416,1024]{1,0:T(8,128)} %get-tuple-element.117.attended, bf16[4,416,1024]{2,1,0:T(8,128)(2,1)} %shard_map.336.refs_2_.cot, bf16[416,1024]{1,0:T(8,128)(2,1)S(1)} %add_convert_fusion.4.mine, ...), custom_call_target="tpu_custom_call" | custom-call | flops 3000000000 | bytes 9000000 | tf_op jit(solution)/shard_map/pallas_call | solution.py:384
  180.7 15.5 %shard_map.346 = (bf16[4,416,1024]{2,1,0:T(8,128)(2,1)}, bf16[4,416,768]{2,1,0:T(8,128)(2,1)}, f32[8,768]{1,0:T(8,128)S(1)}, f32[8,1024]{1,0:T(8,128)S(1)}, bf16...) custom-call(s32[2]{0:T(128)S(1)} %get-tuple-element.111.idx, bf16[416,1024]{1,0:T(8,128)(2,1)S(1)} %get-tuple-element.137.refs_0_, ...), custom_call_target="tpu_custom_call" | custom-call | flops 16000000000 | bytes 48000000 | tf_op jit(solution)/shard_map/pallas_call | solution.py:384
  196.2 3.5 collective-permute-done.20.refs_0_
  202.1 15.8 %shard_map.347 = (bf16[4,416,1024]{2,1,0:T(8,128)(2,1)}, bf16[4,416,768]{2,1,0:T(8,128)(2,1)}, f32[8,768]{1,0:T(8,128)S(1)}, f32[8,1024]{1,0:T(8,128)S(1)}, bf16...) custom-call(s32[2]{0:T(128)S(1)} %get-tuple-element.108.idx, ...), custom_call_target="tpu_custom_call", output_to_operand_aliasing={{0}: (6, {}), {1}: (7, {})} | custom-call | flops 16000000000 | bytes 48000000 | tf_op jit(solution)/shard_map/pallas_call | solution.py:384
  223.6 8.5 %shard_map.348 = (bf16[512,512]{1,0:T(8,128)(2,1)S(1)}, bf16[512,512]{1,0:T(8,128)(2,1)S(1)}, bf16[512,640]{1,0:T(8,128)(2,1)S(1)}, bf16[512,640]{1,0:T(8,128)(2,1)}) custom-call(s32[1]{0:T(128)S(6)} %select_n.12.idx, bf16[1664,1024]{1,0:T(8,128)(2,1)} %bitcast.117, bf16[1664,768]{1,0:T(8,128)(2,1)} %bitcast.118, bf16[1664,1024]{1,0:T(8,128)(2,1)} %bitcast.113, ...), custom_call_target="tpu_custom_call" | custom-call | flops 10000000000 | bytes 30000000 | tf_op jit(solution)/shard_map/pallas_call | solution.py:384
  235.9 7.3 %collective-permute-done.23.theirs = bf16[416,1024]{1,0:T(8,128)(2,1)S(1)} collective-permute-done((bf16[416,1024]{1,0:T(8,128)(2,1)S(1)}, bf16[416,1024]{1,0:T(8,128)(2,1)S(1)}, u32[]{:S(2)}, u32[]{:S(2)}) %collective-permute-start.23) | collective-permute-done | bytes 852000 | tf_op jit(solution)/shard_map/ppermute | solution.py:620
  243.2 3.4 shard_map.349.refs_0_
  251.0 4.4 %collective-permute-done.29.given = bf16[512,640]{1,0:T(8,128)(2,1)} collective-permute-done((bf16[512,640]{1,0:T(8,128)(2,1)}, bf16[512,640]{1,0:T(8,128)(2,1)}, u32[]{:S(2)}, u32[]{:S(2)}) %collective-permute-start.29) | collective-permute-done | bytes 655392 | tf_op jit(solution)/shard_map/ppermute | solution.py:632
  259.3 3.8 %reduce-scatter.2.cloned.1.call-done.grad.turned_grad = bf16[128,2048]{1,0:T(8,128)(2,1)} async-done(((bf16[1024,2048]{1,0:T(8,128)(2,1)}), bf16[128,2048]{1,0:T(8,128)(2,1)}) %reduce-scatter.2.cloned.1.call-update) | async-done | bytes 524304 | tf_op jit(solution)/shard_map/reduce_scatter | solution.py:757
  265.3 3.1 shard_map.351
  268.7 16.7 %collective-permute-done.19 = bf16[416,1024]{1,0:T(8,128)(2,1)} collective-permute-done((bf16[416,1024]{1,0:T(8,128)(2,1)}, bf16[416,1024]{1,0:T(8,128)(2,1)}, u32[]{:S(2)}, u32[]{:S(2)}) %collective-permute-start.19) | collective-permute-done | bytes 852000 | tf_op jit(solution)/shard_map/ppermute | solution.py:620
  289.1 5.3 %shard_map.352 = f32[1576,1024]{1,0:T(8,128)} custom-call(s32[4]{0:T(128)S(1)} %iota_xor_fusion.1.idx, bf16[416,1024]{1,0:T(8,128)(2,1)} %shard_map.349.refs_0_, bf16[416,1024]{1,0:T(8,128)(2,1)} %collective-permute-done.27.refs_1_, bf16[416,1024]{1,0:T(8,128)(2,1)} %collective-permute-done.28.refs_2_, bf16[416,1024]{1,0:T(8,128)(2,1)S(1)} %collective-permute-done.30.refs_3_), custom_call_target="tpu_custom_call" | custom-call | flops 4000000000 | bytes 12000000 | tf_op jit(solution)/shard_map/pallas_call | solution.py:384
  294.4 12.5 %collective-permute-done.25.refs_2_ = bf16[416,1024]{1,0:T(8,128)(2,1)S(1)} collective-permute-done((bf16[416,1024]{1,0:T(8,128)(2,1)S(1)}, bf16[416,1024]{1,0:T(8,128)(2,1)S(1)}, u32[]{:S(2)}, u32[]{:S(2)}) %collective-permute-start.25) | collective-permute-done | bytes 852000 | tf_op jit(solution)/shard_map/ppermute | solution.py:620
  310.7 4.1 %collective-permute-start.37 = (bf16[128,640]{1,0:T(8,128)(2,1)S(1)}, bf16[128,640]{1,0:T(8,128)(2,1)S(1)}, u32[]{:S(2)}, u32[]{:S(2)}) collective-permute-start(bf16[128,640]{1,0:T(8,128)(2,1)S(1)} %get-tuple-element.179), channel_id=1, source_target_pairs={{0,16},{4,20},{8,24},{12,28},{16,0},{20,4},{24,8},{28,12},{1,17},{... | collective-permute-start | bytes 491528 | tf_op jit(solution)/shard_map/ppermute | solution.py:632
  314.7 6.5 %collective-permute-done.32.given = bf16[512,512]{1,0:T(8,128)(2,1)S(1)} collective-permute-done((bf16[512,512]{1,0:T(8,128)(2,1)S(1)}, bf16[512,512]{1,0:T(8,128)(2,1)S(1)}, u32[]{:S(2)}, u32[]{:S(2)}) %collective-permute-start.32) | collective-permute-done | bytes 524320 | tf_op jit(solution)/shard_map/ppermute | solution.py:632
  321.3 6.2 %collective-permute-start.38 = (bf16[128,640]{1,0:T(8,128)(2,1)S(1)}, bf16[128,640]{1,0:T(8,128)(2,1)S(1)}, u32[]{:S(2)}, u32[]{:S(2)}) collective-permute-start(bf16[128,640]{1,0:T(8,128)(2,1)S(1)} %get-tuple-element.180), channel_id=1, source_target_pairs={{0,24},{4,28},{8,16},{12,20},{16,8},{20,12},{24,0},{28,4},{1,25},{... | collective-permute-start | bytes 491528 | tf_op jit(solution)/shard_map/ppermute | solution.py:632
  328.3 3.9 %collective-permute-start.35 = (bf16[128,512]{1,0:T(8,128)(2,1)S(1)}, bf16[128,512]{1,0:T(8,128)(2,1)S(1)}, u32[]{:S(2)}, u32[]{:S(2)}) collective-permute-start(bf16[128,512]{1,0:T(8,128)(2,1)S(1)} %get-tuple-element.176), channel_id=1, source_target_pairs={{0,24},{4,28},{8,16},{12,20},{16,8},{20,12},{24,0},{28,4},{1,25},{... | collective-permute-start | bytes 393224 | tf_op jit(solution)/shard_map/ppermute | solution.py:632
  332.2 3.0 shard_map.353
  336.3 5.8 %collective-permute-done.34.refs_2_ = bf16[128,512]{1,0:T(8,128)(2,1)S(1)} collective-permute-done((bf16[128,512]{1,0:T(8,128)(2,1)S(1)}, bf16[128,512]{1,0:T(8,128)(2,1)S(1)}, u32[]{:S(2)}, u32[]{:S(2)}) %collective-permute-start.34) | collective-permute-done | bytes 131104 | tf_op jit(solution)/shard_map/ppermute | solution.py:632
  (232 shorter events, 92.3 us)
Async XLA Ops:
  7.2 106.3 %all-gather.2.cloned.1.call-start = ((), (), s32[]{:S(2)}) async-start(), calls=%async_computation.1 | async-start | bytes 4718592 | tf_op jit(solution)/shard_map/all_gather | solution.py:717
  11.3 10.5 %collective-permute-start.1 = (bf16[128,1152]{1,0:T(8,128)(2,1)S(1)}, bf16[128,1152]{1,0:T(8,128)(2,1)S(1)}, u32[]{:S(2)}, u32[]{:S(2)}) collective-permute-start(bf16[128,1152]{1,0:T(8,128)(2,1)S(1)} %shard_map.337.refs_0_), channel_id=1, source_target_pairs={{0,8},{4,12},{8,0},{12,4},{16,24},{20,28},{24,16},{28,20},{1,9},{5... | collective-permute-start | bytes 884744 | tf_op jit(solution)/shard_map/ppermute | solution.py:632
  14.5 16.7 %collective-permute-start.5 = (bf16[128,1152]{1,0:T(8,128)(2,1)S(1)}, bf16[128,1152]{1,0:T(8,128)(2,1)S(1)}, u32[]{:S(2)}, u32[]{:S(2)}) collective-permute-start(bf16[128,1152]{1,0:T(8,128)(2,1)S(1)} %shard_map.337.refs_0_), channel_id=1, source_target_pairs={{0,24},{4,28},{8,16},{12,20},{16,8},{20,12},{24,0},{28,4},{1,25},{... | collective-permute-start | bytes 884744 | tf_op jit(solution)/shard_map/ppermute | solution.py:632
  16.9 33.6 %collective-permute-start.3 = (bf16[128,1152]{1,0:T(8,128)(2,1)S(1)}, bf16[128,1152]{1,0:T(8,128)(2,1)S(1)}, u32[]{:S(2)}, u32[]{:S(2)}) collective-permute-start(bf16[128,1152]{1,0:T(8,128)(2,1)S(1)} %shard_map.337.refs_0_), channel_id=1, source_target_pairs={{0,16},{4,20},{8,24},{12,28},{16,0},{20,4},{24,8},{28,12},{1,17},{... | collective-permute-start | bytes 884744 | tf_op jit(solution)/shard_map/ppermute | solution.py:632
  17.0 39.9 %collective-permute-start = (bf16[128,1152]{1,0:T(8,128)(2,1)S(1)}, bf16[128,1152]{1,0:T(8,128)(2,1)S(1)}, u32[]{:S(2)}, u32[]{:S(2)}) collective-permute-start(bf16[128,1152]{1,0:T(8,128)(2,1)S(1)} %shard_map.337.refs_0_), channel_id=1, source_target_pairs={{0,4},{4,0},{8,12},{12,8},{16,20},{20,16},{24,28},{28,24},{1,5},{5... | collective-permute-start | bytes 884744 | tf_op jit(solution)/shard_map/ppermute | solution.py:632
  21.9 241.2 %reduce-scatter.2.cloned.1.call-start = ((), (), s32[]{:S(2)}) async-start(), calls=%async_computation.2 | async-start | bytes 4718592 | tf_op jit(solution)/shard_map/reduce_scatter | solution.py:757
  26.5 31.2 %collective-permute-start.2 = (bf16[128,1152]{1,0:T(8,128)(2,1)S(1)}, bf16[128,1152]{1,0:T(8,128)(2,1)S(1)}, u32[]{:S(2)}, u32[]{:S(2)}) collective-permute-start(bf16[128,1152]{1,0:T(8,128)(2,1)S(1)} %collective-permute-done.1.refs_2_), channel_id=1, source_target_pairs={{0,4},{4,0},{8,12},{12,8},{16,20},{20,16},{24,28},{28,24},{1,5},{5... | collective-permute-start | bytes 884744 | tf_op jit(solution)/shard_map/ppermute | solution.py:632
  31.2 25.8 %collective-permute-start.6 = (bf16[128,1152]{1,0:T(8,128)(2,1)S(1)}, bf16[128,1152]{1,0:T(8,128)(2,1)S(1)}, u32[]{:S(2)}, u32[]{:S(2)}) collective-permute-start(bf16[128,1152]{1,0:T(8,128)(2,1)S(1)} %collective-permute-done.5.refs_6_), channel_id=1, source_target_pairs={{0,4},{4,0},{8,12},{12,8},{16,20},{20,16},{24,28},{28,24},{1,5},{5... | collective-permute-start | bytes 884744 | tf_op jit(solution)/shard_map/ppermute | solution.py:632
  86.0 21.2 %collective-permute-start.9 = (bf16[416,1024]{1,0:T(8,128)(2,1)S(1)}, bf16[416,1024]{1,0:T(8,128)(2,1)S(1)}, u32[]{:S(2)}, u32[]{:S(2)}) collective-permute-start(bf16[416,1024]{1,0:T(8,128)(2,1)S(1)} %add_convert_fusion.8), channel_id=1, source_target_pairs={{0,2},{1,3},{2,0},{3,1},{4,6},{5,7},{6,4},{7,5},{8,10},{9,11},{10,... | collective-permute-start | bytes 2555912 | tf_op jit(solution)/shard_map/ppermute | solution.py:620
  110.1 21.6 %collective-permute-start.12 = (bf16[416,1024]{1,0:T(8,128)(2,1)}, bf16[416,1024]{1,0:T(8,128)(2,1)S(1)}, u32[]{:S(2)}, u32[]{:S(2)}) collective-permute-start(bf16[416,1024]{1,0:T(8,128)(2,1)} %get-tuple-element.118.refs_0_), channel_id=1, source_target_pairs={{0,2},{1,3},{2,0},{3,1},{4,6},{5,7},{6,4},{7,5},{8,10},{9,11},{10,... | collective-permute-start | bytes 2555912 | tf_op jit(solution)/shard_map/ppermute | solution.py:620
  149.4 19.1 %collective-permute-start.15 = (bf16[416,1024]{1,0:T(8,128)(2,1)}, bf16[416,1024]{1,0:T(8,128)(2,1)}, u32[]{:S(2)}, u32[]{:S(2)}) collective-permute-start(bf16[416,1024]{1,0:T(8,128)(2,1)} %get-tuple-element.129), channel_id=1, source_target_pairs={{0,1},{1,0},{2,3},{3,2},{4,5},{5,4},{6,7},{7,6},{8,9},{9,8},{10,11... | collective-permute-start | bytes 2555912 | tf_op jit(solution)/shard_map/ppermute | solution.py:620
  152.8 21.4 %collective-permute-start.17 = (bf16[416,1024]{1,0:T(8,128)(2,1)}, bf16[416,1024]{1,0:T(8,128)(2,1)}, u32[]{:S(2)}, u32[]{:S(2)}) collective-permute-start(bf16[416,1024]{1,0:T(8,128)(2,1)} %add_convert_fusion.3), channel_id=1, source_target_pairs={{0,2},{1,3},{2,0},{3,1},{4,6},{5,7},{6,4},{7,5},{8,10},{9,11},{10,... | collective-permute-start | bytes 2555912 | tf_op jit(solution)/shard_map/ppermute | solution.py:620
  178.4 21.4 %collective-permute-start.20 = (bf16[416,1024]{1,0:T(8,128)(2,1)S(1)}, bf16[416,1024]{1,0:T(8,128)(2,1)S(1)}, u32[]{:S(2)}, u32[]{:S(2)}) collective-permute-start(bf16[416,1024]{1,0:T(8,128)(2,1)S(1)} %get-tuple-element.137.refs_0_), channel_id=1, source_target_pairs={{0,2},{1,3},{2,0},{3,1},{4,6},{5,7},{6,4},{7,5},{8,10},{9,11},{10,... | collective-permute-start | bytes 2555912 | tf_op jit(solution)/shard_map/ppermute | solution.py:620
  199.7 69.0 %collective-permute-start.11 = (bf16[416,1024]{1,0:T(8,128)(2,1)}, bf16[416,1024]{1,0:T(8,128)(2,1)}, u32[]{:S(2)}, u32[]{:S(2)}) collective-permute-start(bf16[416,1024]{1,0:T(8,128)(2,1)} %get-tuple-element.121), channel_id=1, source_target_pairs={{0,1},{1,0},{2,3},{3,2},{4,5},{5,4},{6,7},{7,6},{8,9},{9,8},{10,11... | collective-permute-start | bytes 2555912 | tf_op jit(solution)/shard_map/ppermute | solution.py:620
  200.2 47.8 %collective-permute-start.14 = (bf16[416,1024]{1,0:T(8,128)(2,1)}, bf16[416,1024]{1,0:T(8,128)(2,1)}, u32[]{:S(2)}, u32[]{:S(2)}) collective-permute-start(bf16[416,1024]{1,0:T(8,128)(2,1)} %get-tuple-element.128), channel_id=1, source_target_pairs={{0,1},{1,0},{2,3},{3,2},{4,5},{5,4},{6,7},{7,6},{8,9},{9,8},{10,11... | collective-permute-start | bytes 2555912 | tf_op jit(solution)/shard_map/ppermute | solution.py:620
  200.3 34.1 %collective-permute-start.26 = (bf16[416,1024]{1,0:T(8,128)(2,1)}, bf16[416,1024]{1,0:T(8,128)(2,1)}, u32[]{:S(2)}, u32[]{:S(2)}) collective-permute-start(bf16[416,1024]{1,0:T(8,128)(2,1)} %get-tuple-element.162), channel_id=1, source_target_pairs={{0,1},{1,0},{2,3},{3,2},{4,5},{5,4},{6,7},{7,6},{8,9},{9,8},{10,11... | collective-permute-start | bytes 2555912 | tf_op jit(solution)/shard_map/ppermute | solution.py:620
  222.1 21.0 %collective-permute-start.23 = (bf16[416,1024]{1,0:T(8,128)(2,1)S(1)}, bf16[416,1024]{1,0:T(8,128)(2,1)S(1)}, u32[]{:S(2)}, u32[]{:S(2)}) collective-permute-start(bf16[416,1024]{1,0:T(8,128)(2,1)S(1)} %add_convert_fusion.1), channel_id=1, source_target_pairs={{0,2},{1,3},{2,0},{3,1},{4,6},{5,7},{6,4},{7,5},{8,10},{9,11},{10,... | collective-permute-start | bytes 2555912 | tf_op jit(solution)/shard_map/ppermute | solution.py:620
  233.0 22.5 %collective-permute-start.29 = (bf16[512,640]{1,0:T(8,128)(2,1)}, bf16[512,640]{1,0:T(8,128)(2,1)}, u32[]{:S(2)}, u32[]{:S(2)}) collective-permute-start(bf16[512,640]{1,0:T(8,128)(2,1)} %get-tuple-element.164), channel_id=1, source_target_pairs={{0,4},{4,0},{8,12},{12,8},{16,20},{20,16},{24,28},{28,24},{1,5},{5... | collective-permute-start | bytes 1966088 | tf_op jit(solution)/shard_map/ppermute | solution.py:632
  246.6 22.1 %collective-permute-start.28 = (bf16[416,1024]{1,0:T(8,128)(2,1)}, bf16[416,1024]{1,0:T(8,128)(2,1)}, u32[]{:S(2)}, u32[]{:S(2)}) collective-permute-start(bf16[416,1024]{1,0:T(8,128)(2,1)} %shard_map.349.refs_0_), channel_id=1, source_target_pairs={{0,2},{1,3},{2,0},{3,1},{4,6},{5,7},{6,4},{7,5},{8,10},{9,11},{10,... | collective-permute-start | bytes 2555912 | tf_op jit(solution)/shard_map/ppermute | solution.py:620
  250.5 34.9 %collective-permute-start.19 = (bf16[416,1024]{1,0:T(8,128)(2,1)}, bf16[416,1024]{1,0:T(8,128)(2,1)}, u32[]{:S(2)}, u32[]{:S(2)}) collective-permute-start(bf16[416,1024]{1,0:T(8,128)(2,1)} %add_convert_fusion.5), channel_id=1, source_target_pairs={{0,2},{1,3},{2,0},{3,1},{4,6},{5,7},{6,4},{7,5},{8,10},{9,11},{10,... | collective-permute-start | bytes 2555912 | tf_op jit(solution)/shard_map/ppermute | solution.py:620
  259.3 29.9 %collective-permute-start.27 = (bf16[416,1024]{1,0:T(8,128)(2,1)}, bf16[416,1024]{1,0:T(8,128)(2,1)}, u32[]{:S(2)}, u32[]{:S(2)}) collective-permute-start(bf16[416,1024]{1,0:T(8,128)(2,1)} %shard_map.349.refs_0_), channel_id=1, source_target_pairs={{0,1},{1,0},{2,3},{3,2},{4,5},{5,4},{6,7},{7,6},{8,9},{9,8},{10,11... | collective-permute-start | bytes 2555912 | tf_op jit(solution)/shard_map/ppermute | solution.py:620
  268.7 20.4 %collective-permute-start.30 = (bf16[416,1024]{1,0:T(8,128)(2,1)}, bf16[416,1024]{1,0:T(8,128)(2,1)S(1)}, u32[]{:S(2)}, u32[]{:S(2)}) collective-permute-start(bf16[416,1024]{1,0:T(8,128)(2,1)} %collective-permute-done.28.refs_2_), channel_id=1, source_target_pairs={{0,1},{1,0},{2,3},{3,2},{4,5},{5,4},{6,7},{7,6},{8,9},{9,8},{10,11... | collective-permute-start | bytes 2555912 | tf_op jit(solution)/shard_map/ppermute | solution.py:620
  287.5 19.4 %collective-permute-start.25 = (bf16[416,1024]{1,0:T(8,128)(2,1)S(1)}, bf16[416,1024]{1,0:T(8,128)(2,1)S(1)}, u32[]{:S(2)}, u32[]{:S(2)}) collective-permute-start(bf16[416,1024]{1,0:T(8,128)(2,1)S(1)} %add_convert_fusion.2.refs_0_), channel_id=1, source_target_pairs={{0,2},{1,3},{2,0},{3,1},{4,6},{5,7},{6,4},{7,5},{8,10},{9,11},{10,... | collective-permute-start | bytes 2555912 | tf_op jit(solution)/shard_map/ppermute | solution.py:620
  289.1 38.6 %collective-permute-start.24 = (bf16[416,1024]{1,0:T(8,128)(2,1)S(1)}, bf16[416,1024]{1,0:T(8,128)(2,1)S(1)}, u32[]{:S(2)}, u32[]{:S(2)}) collective-permute-start(bf16[416,1024]{1,0:T(8,128)(2,1)S(1)} %add_convert_fusion.2.refs_0_), channel_id=1, source_target_pairs={{0,1},{1,0},{2,3},{3,2},{4,5},{5,4},{6,7},{7,6},{8,9},{9,8},{10,11... | collective-permute-start | bytes 2555912 | tf_op jit(solution)/shard_map/ppermute | solution.py:620
  306.9 21.4 %collective-permute-start.31 = (bf16[416,1024]{1,0:T(8,128)(2,1)S(1)}, bf16[416,1024]{1,0:T(8,128)(2,1)S(1)}, u32[]{:S(2)}, u32[]{:S(2)}) collective-permute-start(bf16[416,1024]{1,0:T(8,128)(2,1)S(1)} %collective-permute-done.25.refs_2_), channel_id=1, source_target_pairs={{0,1},{1,0},{2,3},{3,2},{4,5},{5,4},{6,7},{7,6},{8,9},{9,8},{10,11... | collective-permute-start | bytes 2555912 | tf_op jit(solution)/shard_map/ppermute | solution.py:620
  306.9 14.3 %collective-permute-start.32 = (bf16[512,512]{1,0:T(8,128)(2,1)S(1)}, bf16[512,512]{1,0:T(8,128)(2,1)S(1)}, u32[]{:S(2)}, u32[]{:S(2)}) collective-permute-start(bf16[512,512]{1,0:T(8,128)(2,1)S(1)} %copy-done.25), channel_id=1, source_target_pairs={{0,4},{4,0},{8,12},{12,8},{16,20},{20,16},{24,28},{28,24},{1,5},{5... | collective-permute-start | bytes 1572872 | tf_op jit(solution)/shard_map/ppermute | solution.py:632
  308.5 19.1 %collective-permute-start.36 = (bf16[128,640]{1,0:T(8,128)(2,1)S(1)}, bf16[128,640]{1,0:T(8,128)(2,1)S(1)}, u32[]{:S(2)}, u32[]{:S(2)}) collective-permute-start(bf16[128,640]{1,0:T(8,128)(2,1)S(1)} %copy-done.31), channel_id=1, source_target_pairs={{0,8},{4,12},{8,0},{12,4},{16,24},{20,28},{24,16},{28,20},{1,9},{5... | collective-permute-start | bytes 491528 | tf_op jit(solution)/shard_map/ppermute | solution.py:632
  310.7 24.6 %collective-permute-start.37 = (bf16[128,640]{1,0:T(8,128)(2,1)S(1)}, bf16[128,640]{1,0:T(8,128)(2,1)S(1)}, u32[]{:S(2)}, u32[]{:S(2)}) collective-permute-start(bf16[128,640]{1,0:T(8,128)(2,1)S(1)} %get-tuple-element.179), channel_id=1, source_target_pairs={{0,16},{4,20},{8,24},{12,28},{16,0},{20,4},{24,8},{28,12},{1,17},{... | collective-permute-start | bytes 491528 | tf_op jit(solution)/shard_map/ppermute | solution.py:632
  321.3 14.0 %collective-permute-start.38 = (bf16[128,640]{1,0:T(8,128)(2,1)S(1)}, bf16[128,640]{1,0:T(8,128)(2,1)S(1)}, u32[]{:S(2)}, u32[]{:S(2)}) collective-permute-start(bf16[128,640]{1,0:T(8,128)(2,1)S(1)} %get-tuple-element.180), channel_id=1, source_target_pairs={{0,24},{4,28},{8,16},{12,20},{16,8},{20,12},{24,0},{28,4},{1,25},{... | collective-permute-start | bytes 491528 | tf_op jit(solution)/shard_map/ppermute | solution.py:632
  327.7 8.6 %collective-permute-start.33 = (bf16[128,512]{1,0:T(8,128)(2,1)S(1)}, bf16[128,512]{1,0:T(8,128)(2,1)S(1)}, u32[]{:S(2)}, u32[]{:S(2)}) collective-permute-start(bf16[128,512]{1,0:T(8,128)(2,1)S(1)} %get-tuple-element.174), channel_id=1, source_target_pairs={{0,8},{4,12},{8,0},{12,4},{16,24},{20,28},{24,16},{28,20},{1,9},{5... | collective-permute-start | bytes 393224 | tf_op jit(solution)/shard_map/ppermute | solution.py:632
  327.8 14.3 %collective-permute-start.34 = (bf16[128,512]{1,0:T(8,128)(2,1)S(1)}, bf16[128,512]{1,0:T(8,128)(2,1)S(1)}, u32[]{:S(2)}, u32[]{:S(2)}) collective-permute-start(bf16[128,512]{1,0:T(8,128)(2,1)S(1)} %get-tuple-element.175), channel_id=1, source_target_pairs={{0,16},{4,20},{8,24},{12,28},{16,0},{20,4},{24,8},{28,12},{1,17},{... | collective-permute-start | bytes 393224 | tf_op jit(solution)/shard_map/ppermute | solution.py:632
  328.3 13.7 %collective-permute-start.35 = (bf16[128,512]{1,0:T(8,128)(2,1)S(1)}, bf16[128,512]{1,0:T(8,128)(2,1)S(1)}, u32[]{:S(2)}, u32[]{:S(2)}) collective-permute-start(bf16[128,512]{1,0:T(8,128)(2,1)S(1)} %get-tuple-element.176), channel_id=1, source_target_pairs={{0,24},{4,28},{8,16},{12,20},{16,8},{20,12},{24,0},{28,4},{1,25},{... | collective-permute-start | bytes 393224 | tf_op jit(solution)/shard_map/ppermute | solution.py:632
  (65 other events, 438.1 us)
Sparse Core Ops, SparseCore 0:
  22.0 82.8 all-gather.1
  168.6 94.4 reduce-scatter.1

commit v2 on v1

--- a/solution.py
+++ b/solution.py
@@ -341,7 +341,6 @@
     for c, value in enumerate((one[:, :width], one[:, width:], two[:, :width])):
         adam_store(value, param.at[c], moments.at[:, c], outs[0].at[c], outs[1].at[c], outs[2].at[:, c])
     adam_store(two[:, width : 2 * width].T, turned, turned_moments, *outs[3:6])
-    outs[6][...] = two[:, 2 * width :]
 
 
 def sum_kernel(idx, kept, given, *outs):
@@ -543,15 +542,14 @@
         [wide, beside, wide, wide_two, tall, tall_two],
         [wide, wide, wide_two, tall, tall, tall_two],
         outs,
-        [grads, grads, param, moments, turned, turned_moments],
+        [out_there(v) for v in (grads, grads, param, moments, turned, turned_moments)],
         us=4,
     )
 
 
 def adam_attention(idx, first, second, param, moments, turned, turned_moments):
-    args = list(first) + list(second) + [param, moments, turned, turned_moments]
+    args = list(first) + list(second) + [out_there(v) for v in (param, moments, turned, turned_moments)]
     outs = [sds(v.shape, f32) for v in (param, param, moments, turned, turned, turned_moments)]
-    outs.append(sds((first[0].shape[0], LANES), f32))
     return call(
         functools.partial(adam_attention_kernel, len(first)),
         (1,),
@@ -584,7 +582,7 @@
 
 def pack(idx, inner, outer, vectors, hidden_bias, bias):
     part, width = inner.shape[1:]
-    args = [inner, outer, vectors, hidden_bias.reshape(1, -1), bias]
+    args = [out_there(v) for v in (inner, outer, vectors, hidden_bias.reshape(1, -1), bias)]
     shape = (part, 4 * width + LANES)
     return call(
         pack_kernel,
@@ -792,7 +790,7 @@
         part,
         2 * width,
     )
-    halves = [(kept, shard_swap(given, 1, n_shard)) for kept, given in (grads_one[:2], grads_one[2:])]
+    halves = [(kept, shard_swap(given, 1, n_shard)) for (kept, given) in (grads_one[:2], grads_one[2:])]
 
     theirs = tie(theirs, grads_one[0])
     (token_low,) = rowwise(token_back_kernel, own, [tok, mid, mine, theirs, vec], "qRrrw", [sds(block, bf16)])
@@ -807,15 +805,15 @@
         own, share_two, expand_weight, expand_moments, shrink_weight, shrink_moments
     )
     token_gradient = spread(index, near_t + gather_far(over_t, share_expand), f32)
+    small = functools.reduce(jnp.add, [piece[:n_small, 2 * width :].astype(f32) for piece in [tie(halves[1][0], token_gradient)] + halves[1][1:]])
+    own_vectors = small[:6, :part]
+    swapped = [swap(own_vectors, k, n_tensor) for k in range(1, n_tensor)]
     block_output = spread(index, near_o + gather_far(over_o, token_gradient), bf16)
     first, second = [[tie(half[0], block_output)] + half[1:] for half in halves]
-    share_input, new_input, mom_input, share_output, new_output, mom_output, small = adam_attention(
+    share_input, new_input, mom_input, share_output, new_output, mom_output = adam_attention(
         own, first, second, input_weight, input_moments, output_weight, output_moments
     )
-    own_vectors = small[:6, :part]
-    share_vectors = functools.reduce(
-        jnp.add, [own_vectors] + [swap(own_vectors, k, n_tensor) for k in range(1, n_tensor)]
-    )
+    share_vectors = functools.reduce(jnp.add, [own_vectors] + swapped)
     share_expand_bias = small[6, :part]
     share_bias = small[7:9, : width // n_shard]
 

time: 358 us -> 335 us (0.936)
  waiting for transfers between devices: 120 us -> 104 us
  local copies, waits for them, and re-layouts: 25.9 us -> 19.8 us
  starting transfers between devices: 47.4 us -> 41.8 us
  Pallas kernels: 135 us -> 139 us
    ppermute x27, waiting for transfers between devices: 74.9 us -> 59.7 us  [swap(): return lax.ppermute(value, TENSOR, [(k, k ^ flip) for k in range(size)])]
    unnamed x109 -> x73, local copies, waits for them, and re-layouts: 24.3 us -> 18.2 us
    ppermute x15, starting transfers between devices: 32.1 us -> 26.3 us  [shard_swap(): return lax.ppermute(value, SHARD, [(k, k ^ flip) for k in range(size)])]
    pallas_call x21, Pallas kernels: 135 us -> 139 us  [call(): pl.pallas_call(kernel, grid_spec=pltpu.PrefetchScalarGridSpec(num_scalar_...]
  transfers between devices with their start and end apart: 44 -> 44, of which waited for: 26 -> 21; matrix products, arithmetic and copies ran while one was open for 4% -> 6% of each run, Pallas kernels for 33% -> 36%
where the time goes in v2:
time: 335 us; the launch traced here: 334 us
  Pallas kernels  139 us (41%)
  waiting for transfers between devices  104 us (31%)
  starting transfers between devices  41.8 us (12%)
  local copies, waits for them, and re-layouts  19.8 us (6%)
  other arithmetic  15.6 us (5%)
  between operations  14.6 us (4%)
    pallas_call x21, Pallas kernels, call(): pl.pallas_call(kernel, grid_spec=pltpu.PrefetchScalarGridSpec(num_scalar_...  139 us
    ppermute x27, waiting for transfers between devices, swap(): return lax.ppermute(value, TENSOR, [(k, k ^ flip) for k in range(size)])  59.7 us
    ppermute x15, waiting for transfers between devices, shard_swap(): return lax.ppermute(value, SHARD, [(k, k ^ flip) for k in range(size)])  40.6 us
    ppermute x15, starting transfers between devices, shard_swap(): return lax.ppermute(value, SHARD, [(k, k ^ flip) for k in range(size)])  26.3 us
    unnamed x73, local copies, waits for them, and re-layouts  18.2 us
    ppermute x27, starting transfers between devices, swap(): return lax.ppermute(value, TENSOR, [(k, k ^ flip) for k in range(size)])  15.4 us
    convert_element_type x7, other arithmetic, add_low(): return (left.astype(f32) + right.astype(f32)).astype(bf16)  8.67 us
  transfers between devices with their start and end apart: 44, of which 21 were waited for; matrix products, arithmetic and copies ran while one was open for 6% of the time, Pallas kernels for 36%

profile of v2, /device:TPU:0, one launch (start us, length us, event | category | flops | bytes accessed | tf_op | source)
XLA Modules:
  0.0 334.2 jit_solution(17541536494803650286)
XLA Ops:
  9.4 3.1 collective-permute-start.1
  12.4 2.5 collective-permute-start.5
  20.3 2.6 shard_map.336.refs_2_.cot
  24.4 5.1 %collective-permute-done.5.refs_6_ = bf16[128,1152]{1,0:T(8,128)(2,1)} collective-permute-done((bf16[128,1152]{1,0:T(8,128)(2,1)}, bf16[128,1152]{1,0:T(8,128)(2,1)}, u32[]{:S(2)}, u32[]{:S(2)}) %collective-permute-start.5) | collective-permute-done | bytes 294944 | tf_op jit(solution)/shard_map/ppermute | solution.py:630
  31.0 18.2 %collective-permute-done.3.refs_4_ = bf16[128,1152]{1,0:T(8,128)(2,1)} collective-permute-done((bf16[128,1152]{1,0:T(8,128)(2,1)}, bf16[128,1152]{1,0:T(8,128)(2,1)}, u32[]{:S(2)}, u32[]{:S(2)}) %collective-permute-start.3) | collective-permute-done | bytes 294944 | tf_op jit(solution)/shard_map/ppermute | solution.py:630
  52.7 2.5 shard_map.335.tok.refs_2_
  60.0 10.8 %shard_map.339 = (bf16[4,416,1024]{2,1,0:T(8,128)(2,1)}, bf16[4,416,768]{2,1,0:T(8,128)(2,1)}, bf16[4,416,256]{2,1,0:T(8,128)(2,1)}, bf16[416,1024]{1,0:T(8,128)(2,1)S(1)}, bf16[416,1024]{1,0:T(8,128)(2,1)S(1)}) custom-call(s32[2]{0:T(128)S(1)} %get-tuple-element.108.idx, bf16[4,416,1024]{2,1,0:T(8,128)(2,1)} %shard_map.335.tok.refs_2_, ...), custom_call_target="tpu_custom_call" | custom-call | flops 12000000000 | bytes 36000000 | tf_op jit(solution)/shard_map/pallas_call | solution.py:383
  73.5 10.7 %shard_map.340 = (bf16[4,416,1024]{2,1,0:T(8,128)(2,1)}, bf16[4,416,768]{2,1,0:T(8,128)(2,1)}, bf16[4,416,256]{2,1,0:T(8,128)(2,1)}, bf16[416,1024]{1,0:T(8,128)(2,1)S(1)}, bf16[416,1024]{1,0:T(8,128)(2,1)S(1)}) custom-call(s32[2]{0:T(128)S(1)} %get-tuple-element.111.idx, ...), custom_call_target="tpu_custom_call", output_to_operand_aliasing={{0}: (5, {}), {1}: (6, {}), {2}: (7, {})} | custom-call | flops 12000000000 | bytes 36000000 | tf_op jit(solution)/shard_map/pallas_call | solution.py:383
  86.9 18.7 %collective-permute-done.9.theirs = bf16[416,1024]{1,0:T(8,128)(2,1)S(1)} collective-permute-done((bf16[416,1024]{1,0:T(8,128)(2,1)S(1)}, bf16[416,1024]{1,0:T(8,128)(2,1)S(1)}, u32[]{:S(2)}, u32[]{:S(2)}) %collective-permute-start.9) | collective-permute-done | bytes 852000 | tf_op jit(solution)/shard_map/ppermute | solution.py:618
  105.5 2.8 shard_map.341
  115.2 14.4 %shard_map.342 = (bf16[4,416,1024]{2,1,0:T(8,128)(2,1)}, bf16[4,416,1024]{2,1,0:T(8,128)(2,1)}, bf16[4,416,1024]{2,1,0:T(8,128)(2,1)}, f32[8,1024]{1,0:T(8,128)S...) custom-call(s32[2]{0:T(128)S(1)} %get-tuple-element.111.idx, ...), custom_call_target="tpu_custom_call" | custom-call | flops 16000000000 | bytes 48000000 | tf_op jit(solution)/shard_map/pallas_call | solution.py:383
  133.5 14.1 %shard_map.343 = (bf16[4,416,1024]{2,1,0:T(8,128)(2,1)}, bf16[4,416,1024]{2,1,0:T(8,128)(2,1)}, bf16[4,416,1024]{2,1,0:T(8,128)(2,1)}, f32[8,1024]{1,0:T(8,128)S...) custom-call(s32[2]{0:T(128)S(1)} %get-tuple-element.108.idx, ...), custom_call_target="tpu_custom_call", output_to_operand_aliasing={{0}: (6, {}), {1}: (7, {}), {2}: (8, {})} | custom-call | flops 16000000000 | bytes 48000000 | tf_op jit(solution)/shard_map/pallas_call | solution.py:383
  152.7 12.1 %shard_map.344 = bf16[1024,2048]{1,0:T(8,128)(2,1)S(1)} custom-call(s32[1]{0:T(128)S(1)} %bitcast.103, bf16[1664,1024]{1,0:T(8,128)(2,1)} %bitcast.114, bf16[1664,1024]{1,0:T(8,128)(2,1)} %bitcast.116, bf16[1664,1024]{1,0:T(8,128)(2,1)} %bitcast.112, bf16[1664,1024]{1,0:T(8,128)(2,1)} %bitcast.115), custom_call_target="tpu_custom_call" | custom-call | flops 14000000000 | bytes 42000000 | tf_op jit(solution)/shard_map/pallas_call | solution.py:383
  168.3 4.2 %collective-permute-done.17.theirs = bf16[416,1024]{1,0:T(8,128)(2,1)} collective-permute-done((bf16[416,1024]{1,0:T(8,128)(2,1)}, bf16[416,1024]{1,0:T(8,128)(2,1)}, u32[]{:S(2)}, u32[]{:S(2)}) %collective-permute-start.17) | collective-permute-done | bytes 852000 | tf_op jit(solution)/shard_map/ppermute | solution.py:618
  172.5 4.2 %shard_map.345 = (f32[416,1024]{1,0:T(8,128)}, bf16[416,1024]{1,0:T(8,128)(2,1)S(1)}, f32[8,1024]{1,0:T(8,128)S(1)}) custom-call(s32[1]{0:T(128)S(1)} %bitcast.104, f32[416,1024]{1,0:T(8,128)} %get-tuple-element.117.attended, bf16[4,416,1024]{2,1,0:T(8,128)(2,1)} %shard_map.336.refs_2_.cot, bf16[416,1024]{1,0:T(8,128)(2,1)S(1)} %add_convert_fusion.4.mine, ...), custom_call_target="tpu_custom_call" | custom-call | flops 3000000000 | bytes 9000000 | tf_op jit(solution)/shard_map/pallas_call | solution.py:383
  179.1 15.5 %shard_map.346 = (bf16[4,416,1024]{2,1,0:T(8,128)(2,1)}, bf16[4,416,768]{2,1,0:T(8,128)(2,1)}, f32[8,768]{1,0:T(8,128)S(1)}, f32[8,1024]{1,0:T(8,128)S(1)}, bf16...) custom-call(s32[2]{0:T(128)S(1)} %get-tuple-element.111.idx, bf16[416,1024]{1,0:T(8,128)(2,1)S(1)} %get-tuple-element.137.refs_0_, ...), custom_call_target="tpu_custom_call" | custom-call | flops 16000000000 | bytes 48000000 | tf_op jit(solution)/shard_map/pallas_call | solution.py:383
  194.6 3.5 %collective-permute-done.20.refs_0_ = bf16[416,1024]{1,0:T(8,128)(2,1)S(1)} collective-permute-done((bf16[416,1024]{1,0:T(8,128)(2,1)S(1)}, bf16[416,1024]{1,0:T(8,128)(2,1)S(1)}, u32[]{:S(2)}, u32[]{:S(2)}) %collective-permute-start.20) | collective-permute-done | bytes 852000 | tf_op jit(solution)/shard_map/ppermute | solution.py:618
  200.5 15.7 %shard_map.347 = (bf16[4,416,1024]{2,1,0:T(8,128)(2,1)}, bf16[4,416,768]{2,1,0:T(8,128)(2,1)}, f32[8,768]{1,0:T(8,128)S(1)}, f32[8,1024]{1,0:T(8,128)S(1)}, bf16...) custom-call(s32[2]{0:T(128)S(1)} %get-tuple-element.108.idx, ...), custom_call_target="tpu_custom_call", output_to_operand_aliasing={{0}: (6, {}), {1}: (7, {})} | custom-call | flops 16000000000 | bytes 48000000 | tf_op jit(solution)/shard_map/pallas_call | solution.py:383
  222.0 8.5 %shard_map.348 = (bf16[512,512]{1,0:T(8,128)(2,1)S(1)}, bf16[512,512]{1,0:T(8,128)(2,1)S(1)}, bf16[512,640]{1,0:T(8,128)(2,1)S(1)}, bf16[512,640]{1,0:T(8,128)(2,1)}) custom-call(s32[1]{0:T(128)S(6)} %select_n.12.idx, bf16[1664,1024]{1,0:T(8,128)(2,1)} %bitcast.117, bf16[1664,768]{1,0:T(8,128)(2,1)} %bitcast.118, bf16[1664,1024]{1,0:T(8,128)(2,1)} %bitcast.113, ...), custom_call_target="tpu_custom_call" | custom-call | flops 10000000000 | bytes 30000000 | tf_op jit(solution)/shard_map/pallas_call | solution.py:383
  234.3 7.2 %collective-permute-done.23.theirs = bf16[416,1024]{1,0:T(8,128)(2,1)S(1)} collective-permute-done((bf16[416,1024]{1,0:T(8,128)(2,1)S(1)}, bf16[416,1024]{1,0:T(8,128)(2,1)S(1)}, u32[]{:S(2)}, u32[]{:S(2)}) %collective-permute-start.23) | collective-permute-done | bytes 852000 | tf_op jit(solution)/shard_map/ppermute | solution.py:618
  241.5 2.7 shard_map.349.refs_0_
  248.7 5.1 %collective-permute-done.29.given = bf16[512,640]{1,0:T(8,128)(2,1)} collective-permute-done((bf16[512,640]{1,0:T(8,128)(2,1)}, bf16[512,640]{1,0:T(8,128)(2,1)}, u32[]{:S(2)}, u32[]{:S(2)}) %collective-permute-start.29) | collective-permute-done | bytes 655392 | tf_op jit(solution)/shard_map/ppermute | solution.py:630
  258.1 3.3 reduce-scatter.2.cloned.1.call-done.grad.turned_grad
  261.4 5.2 %shard_map.351 = (f32[128,1024]{1,0:T(8,128)}, f32[128,1024]{1,0:T(8,128)}, f32[2,128,1024]{2,1,0:T(8,128)}, f32[1024,128]{1,0:T(8,128)}, f32[1024,128]{1,0:T(8,128)}, /*index=5*/f32[2,1024,128]{2,1,0:T(8,128)}) custom-call(s32[1]{0:T(128)S(1)} %bitcast.106, bf16[128,2048]{1,0:T(8,128)(2,1)} %reduce-scatter.2.cloned.1.call-done.grad.turned_grad, ...), custom_call_target="tpu_custom_call" | custom-call | flops 4000000000 | bytes 12000000 | tf_op jit(solution)/shard_map/pallas_call | solution.py:383
  267.8 15.0 %collective-permute-done.19 = bf16[416,1024]{1,0:T(8,128)(2,1)} collective-permute-done((bf16[416,1024]{1,0:T(8,128)(2,1)}, bf16[416,1024]{1,0:T(8,128)(2,1)}, u32[]{:S(2)}, u32[]{:S(2)}) %collective-permute-start.19) | collective-permute-done | bytes 852000 | tf_op jit(solution)/shard_map/ppermute | solution.py:618
  288.7 4.1 %collective-permute-start.37 = (bf16[128,640]{1,0:T(8,128)(2,1)S(1)}, bf16[128,640]{1,0:T(8,128)(2,1)S(1)}, u32[]{:S(2)}, u32[]{:S(2)}) collective-permute-start(bf16[128,640]{1,0:T(8,128)(2,1)S(1)} %copy-done.15), channel_id=1, source_target_pairs={{0,16},{4,20},{8,24},{12,28},{16,0},{20,4},{24,8},{28,12},{1,17},{... | collective-permute-start | bytes 491528 | tf_op jit(solution)/shard_map/ppermute | solution.py:630
  293.2 5.0 %shard_map.352 = f32[1576,1024]{1,0:T(8,128)} custom-call(s32[4]{0:T(128)S(1)} %iota_xor_fusion.1.idx, bf16[416,1024]{1,0:T(8,128)(2,1)S(1)} %shard_map.349.refs_0_, bf16[416,1024]{1,0:T(8,128)(2,1)} %collective-permute-done.27.refs_1_, bf16[416,1024]{1,0:T(8,128)(2,1)S(1)} %collective-permute-done.28.refs_2_, ...), custom_call_target="tpu_custom_call" | custom-call | flops 4000000000 | bytes 12000000 | tf_op jit(solution)/shard_map/pallas_call | solution.py:383
  298.2 5.6 %collective-permute-done.37.refs_6_ = bf16[128,640]{1,0:T(8,128)(2,1)S(1)} collective-permute-done((bf16[128,640]{1,0:T(8,128)(2,1)S(1)}, bf16[128,640]{1,0:T(8,128)(2,1)S(1)}, u32[]{:S(2)}, u32[]{:S(2)}) %collective-permute-start.37) | collective-permute-done | bytes 163872 | tf_op jit(solution)/shard_map/ppermute | solution.py:630
  310.8 3.2 collective-permute-start.34
  315.3 3.0 shard_map.353
  318.3 5.7 %collective-permute-done.34.refs_2_ = bf16[128,512]{1,0:T(8,128)(2,1)S(1)} collective-permute-done((bf16[128,512]{1,0:T(8,128)(2,1)S(1)}, bf16[128,512]{1,0:T(8,128)(2,1)S(1)}, u32[]{:S(2)}, u32[]{:S(2)}) %collective-permute-start.34) | collective-permute-done | bytes 131104 | tf_op jit(solution)/shard_map/ppermute | solution.py:630
  324.0 3.3 shard_map.355
  (197 shorter events, 82.1 us)
Async XLA Ops:
  7.2 104.7 %all-gather.2.cloned.1.call-start = ((), (), s32[]{:S(2)}) async-start(), calls=%async_computation.1 | async-start | bytes 4718592 | tf_op jit(solution)/shard_map/all_gather | solution.py:715
  9.4 10.9 %collective-permute-start.1 = (bf16[128,1152]{1,0:T(8,128)(2,1)}, bf16[128,1152]{1,0:T(8,128)(2,1)}, u32[]{:S(2)}, u32[]{:S(2)}) collective-permute-start(bf16[128,1152]{1,0:T(8,128)(2,1)} %shard_map.337.refs_0_), channel_id=1, source_target_pairs={{0,8},{4,12},{8,0},{12,4},{16,24},{20,28},{24,16},{28,20},{1,9},{5... | collective-permute-start | bytes 884744 | tf_op jit(solution)/shard_map/ppermute | solution.py:630
  12.4 17.1 %collective-permute-start.5 = (bf16[128,1152]{1,0:T(8,128)(2,1)}, bf16[128,1152]{1,0:T(8,128)(2,1)}, u32[]{:S(2)}, u32[]{:S(2)}) collective-permute-start(bf16[128,1152]{1,0:T(8,128)(2,1)} %shard_map.337.refs_0_), channel_id=1, source_target_pairs={{0,24},{4,28},{8,16},{12,20},{16,8},{20,12},{24,0},{28,4},{1,25},{... | collective-permute-start | bytes 884744 | tf_op jit(solution)/shard_map/ppermute | solution.py:630
  14.9 34.3 %collective-permute-start.3 = (bf16[128,1152]{1,0:T(8,128)(2,1)}, bf16[128,1152]{1,0:T(8,128)(2,1)}, u32[]{:S(2)}, u32[]{:S(2)}) collective-permute-start(bf16[128,1152]{1,0:T(8,128)(2,1)} %shard_map.337.refs_0_), channel_id=1, source_target_pairs={{0,16},{4,20},{8,24},{12,28},{16,0},{20,4},{24,8},{28,12},{1,17},{... | collective-permute-start | bytes 884744 | tf_op jit(solution)/shard_map/ppermute | solution.py:630
  15.0 40.2 %collective-permute-start = (bf16[128,1152]{1,0:T(8,128)(2,1)}, bf16[128,1152]{1,0:T(8,128)(2,1)}, u32[]{:S(2)}, u32[]{:S(2)}) collective-permute-start(bf16[128,1152]{1,0:T(8,128)(2,1)} %shard_map.337.refs_0_), channel_id=1, source_target_pairs={{0,4},{4,0},{8,12},{12,8},{16,20},{20,16},{24,28},{28,24},{1,5},{5... | collective-permute-start | bytes 884744 | tf_op jit(solution)/shard_map/ppermute | solution.py:630
  20.3 241.1 %reduce-scatter.2.cloned.1.call-start = ((), (), s32[]{:S(2)}) async-start(), calls=%async_computation.2 | async-start | bytes 4718592 | tf_op jit(solution)/shard_map/reduce_scatter | solution.py:755
  23.0 33.1 %collective-permute-start.2 = (bf16[128,1152]{1,0:T(8,128)(2,1)}, bf16[128,1152]{1,0:T(8,128)(2,1)S(1)}, u32[]{:S(2)}, u32[]{:S(2)}) collective-permute-start(bf16[128,1152]{1,0:T(8,128)(2,1)} %collective-permute-done.1.refs_2_), channel_id=1, source_target_pairs={{0,4},{4,0},{8,12},{12,8},{16,20},{20,16},{24,28},{28,24},{1,5},{5... | collective-permute-start | bytes 884744 | tf_op jit(solution)/shard_map/ppermute | solution.py:630
  29.5 25.7 %collective-permute-start.6 = (bf16[128,1152]{1,0:T(8,128)(2,1)}, bf16[128,1152]{1,0:T(8,128)(2,1)S(1)}, u32[]{:S(2)}, u32[]{:S(2)}) collective-permute-start(bf16[128,1152]{1,0:T(8,128)(2,1)} %collective-permute-done.5.refs_6_), channel_id=1, source_target_pairs={{0,4},{4,0},{8,12},{12,8},{16,20},{20,16},{24,28},{28,24},{1,5},{5... | collective-permute-start | bytes 884744 | tf_op jit(solution)/shard_map/ppermute | solution.py:630
  84.3 21.2 %collective-permute-start.9 = (bf16[416,1024]{1,0:T(8,128)(2,1)S(1)}, bf16[416,1024]{1,0:T(8,128)(2,1)S(1)}, u32[]{:S(2)}, u32[]{:S(2)}) collective-permute-start(bf16[416,1024]{1,0:T(8,128)(2,1)S(1)} %add_convert_fusion.8), channel_id=1, source_target_pairs={{0,2},{1,3},{2,0},{3,1},{4,6},{5,7},{6,4},{7,5},{8,10},{9,11},{10,... | collective-permute-start | bytes 2555912 | tf_op jit(solution)/shard_map/ppermute | solution.py:618
  108.4 21.6 %collective-permute-start.12 = (bf16[416,1024]{1,0:T(8,128)(2,1)}, bf16[416,1024]{1,0:T(8,128)(2,1)S(1)}, u32[]{:S(2)}, u32[]{:S(2)}) collective-permute-start(bf16[416,1024]{1,0:T(8,128)(2,1)} %get-tuple-element.118.refs_0_), channel_id=1, source_target_pairs={{0,2},{1,3},{2,0},{3,1},{4,6},{5,7},{6,4},{7,5},{8,10},{9,11},{10,... | collective-permute-start | bytes 2555912 | tf_op jit(solution)/shard_map/ppermute | solution.py:618
  147.7 19.1 %collective-permute-start.15 = (bf16[416,1024]{1,0:T(8,128)(2,1)}, bf16[416,1024]{1,0:T(8,128)(2,1)}, u32[]{:S(2)}, u32[]{:S(2)}) collective-permute-start(bf16[416,1024]{1,0:T(8,128)(2,1)} %get-tuple-element.129), channel_id=1, source_target_pairs={{0,1},{1,0},{2,3},{3,2},{4,5},{5,4},{6,7},{7,6},{8,9},{9,8},{10,11... | collective-permute-start | bytes 2555912 | tf_op jit(solution)/shard_map/ppermute | solution.py:618
  151.2 21.3 %collective-permute-start.17 = (bf16[416,1024]{1,0:T(8,128)(2,1)}, bf16[416,1024]{1,0:T(8,128)(2,1)}, u32[]{:S(2)}, u32[]{:S(2)}) collective-permute-start(bf16[416,1024]{1,0:T(8,128)(2,1)} %add_convert_fusion.3), channel_id=1, source_target_pairs={{0,2},{1,3},{2,0},{3,1},{4,6},{5,7},{6,4},{7,5},{8,10},{9,11},{10,... | collective-permute-start | bytes 2555912 | tf_op jit(solution)/shard_map/ppermute | solution.py:618
  176.7 21.4 %collective-permute-start.20 = (bf16[416,1024]{1,0:T(8,128)(2,1)S(1)}, bf16[416,1024]{1,0:T(8,128)(2,1)S(1)}, u32[]{:S(2)}, u32[]{:S(2)}) collective-permute-start(bf16[416,1024]{1,0:T(8,128)(2,1)S(1)} %get-tuple-element.137.refs_0_), channel_id=1, source_target_pairs={{0,2},{1,3},{2,0},{3,1},{4,6},{5,7},{6,4},{7,5},{8,10},{9,11},{10,... | collective-permute-start | bytes 2555912 | tf_op jit(solution)/shard_map/ppermute | solution.py:618
  198.1 69.7 %collective-permute-start.11 = (bf16[416,1024]{1,0:T(8,128)(2,1)}, bf16[416,1024]{1,0:T(8,128)(2,1)}, u32[]{:S(2)}, u32[]{:S(2)}) collective-permute-start(bf16[416,1024]{1,0:T(8,128)(2,1)} %get-tuple-element.121), channel_id=1, source_target_pairs={{0,1},{1,0},{2,3},{3,2},{4,5},{5,4},{6,7},{7,6},{8,9},{9,8},{10,11... | collective-permute-start | bytes 2555912 | tf_op jit(solution)/shard_map/ppermute | solution.py:618
  198.6 47.1 %collective-permute-start.14 = (bf16[416,1024]{1,0:T(8,128)(2,1)}, bf16[416,1024]{1,0:T(8,128)(2,1)}, u32[]{:S(2)}, u32[]{:S(2)}) collective-permute-start(bf16[416,1024]{1,0:T(8,128)(2,1)} %get-tuple-element.128), channel_id=1, source_target_pairs={{0,1},{1,0},{2,3},{3,2},{4,5},{5,4},{6,7},{7,6},{8,9},{9,8},{10,11... | collective-permute-start | bytes 2555912 | tf_op jit(solution)/shard_map/ppermute | solution.py:618
  198.6 34.2 %collective-permute-start.26 = (bf16[416,1024]{1,0:T(8,128)(2,1)}, bf16[416,1024]{1,0:T(8,128)(2,1)}, u32[]{:S(2)}, u32[]{:S(2)}) collective-permute-start(bf16[416,1024]{1,0:T(8,128)(2,1)} %get-tuple-element.162), channel_id=1, source_target_pairs={{0,1},{1,0},{2,3},{3,2},{4,5},{5,4},{6,7},{7,6},{8,9},{9,8},{10,11... | collective-permute-start | bytes 2555912 | tf_op jit(solution)/shard_map/ppermute | solution.py:618
  220.5 21.0 %collective-permute-start.23 = (bf16[416,1024]{1,0:T(8,128)(2,1)S(1)}, bf16[416,1024]{1,0:T(8,128)(2,1)S(1)}, u32[]{:S(2)}, u32[]{:S(2)}) collective-permute-start(bf16[416,1024]{1,0:T(8,128)(2,1)S(1)} %add_convert_fusion.1), channel_id=1, source_target_pairs={{0,2},{1,3},{2,0},{3,1},{4,6},{5,7},{6,4},{7,5},{8,10},{9,11},{10,... | collective-permute-start | bytes 2555912 | tf_op jit(solution)/shard_map/ppermute | solution.py:618
  231.4 22.4 %collective-permute-start.29 = (bf16[512,640]{1,0:T(8,128)(2,1)}, bf16[512,640]{1,0:T(8,128)(2,1)}, u32[]{:S(2)}, u32[]{:S(2)}) collective-permute-start(bf16[512,640]{1,0:T(8,128)(2,1)} %get-tuple-element.164), channel_id=1, source_target_pairs={{0,4},{4,0},{8,12},{12,8},{16,20},{20,16},{24,28},{28,24},{1,5},{5... | collective-permute-start | bytes 1966088 | tf_op jit(solution)/shard_map/ppermute | solution.py:630
  244.2 22.4 %collective-permute-start.28 = (bf16[416,1024]{1,0:T(8,128)(2,1)S(1)}, bf16[416,1024]{1,0:T(8,128)(2,1)S(1)}, u32[]{:S(2)}, u32[]{:S(2)}) collective-permute-start(bf16[416,1024]{1,0:T(8,128)(2,1)S(1)} %shard_map.349.refs_0_), channel_id=1, source_target_pairs={{0,2},{1,3},{2,0},{3,1},{4,6},{5,7},{6,4},{7,5},{8,10},{9,11},{10,... | collective-permute-start | bytes 2555912 | tf_op jit(solution)/shard_map/ppermute | solution.py:618
  248.1 34.7 %collective-permute-start.19 = (bf16[416,1024]{1,0:T(8,128)(2,1)}, bf16[416,1024]{1,0:T(8,128)(2,1)}, u32[]{:S(2)}, u32[]{:S(2)}) collective-permute-start(bf16[416,1024]{1,0:T(8,128)(2,1)} %add_convert_fusion.5), channel_id=1, source_target_pairs={{0,2},{1,3},{2,0},{3,1},{4,6},{5,7},{6,4},{7,5},{8,10},{9,11},{10,... | collective-permute-start | bytes 2555912 | tf_op jit(solution)/shard_map/ppermute | solution.py:618
  258.1 34.8 %collective-permute-start.27 = (bf16[416,1024]{1,0:T(8,128)(2,1)S(1)}, bf16[416,1024]{1,0:T(8,128)(2,1)}, u32[]{:S(2)}, u32[]{:S(2)}) collective-permute-start(bf16[416,1024]{1,0:T(8,128)(2,1)S(1)} %shard_map.349.refs_0_), channel_id=1, source_target_pairs={{0,1},{1,0},{2,3},{3,2},{4,5},{5,4},{6,7},{7,6},{8,9},{9,8},{10,11... | collective-permute-start | bytes 2555912 | tf_op jit(solution)/shard_map/ppermute | solution.py:618
  266.5 26.6 %collective-permute-start.30 = (bf16[416,1024]{1,0:T(8,128)(2,1)S(1)}, bf16[416,1024]{1,0:T(8,128)(2,1)S(1)}, u32[]{:S(2)}, u32[]{:S(2)}) collective-permute-start(bf16[416,1024]{1,0:T(8,128)(2,1)S(1)} %collective-permute-done.28.refs_2_), channel_id=1, source_target_pairs={{0,1},{1,0},{2,3},{3,2},{4,5},{5,4},{6,7},{7,6},{8,9},{9,8},{10,11... | collective-permute-start | bytes 2555912 | tf_op jit(solution)/shard_map/ppermute | solution.py:618
  266.6 22.0 %collective-permute-start.32 = (bf16[512,512]{1,0:T(8,128)(2,1)S(1)}, bf16[512,512]{1,0:T(8,128)(2,1)S(1)}, u32[]{:S(2)}, u32[]{:S(2)}) collective-permute-start(bf16[512,512]{1,0:T(8,128)(2,1)S(1)} %copy-done.11), channel_id=1, source_target_pairs={{0,4},{4,0},{8,12},{12,8},{16,20},{20,16},{24,28},{28,24},{1,5},{5... | collective-permute-start | bytes 1572872 | tf_op jit(solution)/shard_map/ppermute | solution.py:630
  285.0 21.1 %collective-permute-start.25 = (bf16[416,1024]{1,0:T(8,128)(2,1)S(1)}, bf16[416,1024]{1,0:T(8,128)(2,1)S(1)}, u32[]{:S(2)}, u32[]{:S(2)}) collective-permute-start(bf16[416,1024]{1,0:T(8,128)(2,1)S(1)} %add_convert_fusion.2.refs_0_), channel_id=1, source_target_pairs={{0,2},{1,3},{2,0},{3,1},{4,6},{5,7},{6,4},{7,5},{8,10},{9,11},{10,... | collective-permute-start | bytes 2555912 | tf_op jit(solution)/shard_map/ppermute | solution.py:618
  286.6 11.6 %collective-permute-start.36 = (bf16[128,640]{1,0:T(8,128)(2,1)S(1)}, bf16[128,640]{1,0:T(8,128)(2,1)S(1)}, u32[]{:S(2)}, u32[]{:S(2)}) collective-permute-start(bf16[128,640]{1,0:T(8,128)(2,1)S(1)} %copy-done.17), channel_id=1, source_target_pairs={{0,8},{4,12},{8,0},{12,4},{16,24},{20,28},{24,16},{28,20},{1,9},{5... | collective-permute-start | bytes 491528 | tf_op jit(solution)/shard_map/ppermute | solution.py:630
  288.7 15.1 %collective-permute-start.37 = (bf16[128,640]{1,0:T(8,128)(2,1)S(1)}, bf16[128,640]{1,0:T(8,128)(2,1)S(1)}, u32[]{:S(2)}, u32[]{:S(2)}) collective-permute-start(bf16[128,640]{1,0:T(8,128)(2,1)S(1)} %copy-done.15), channel_id=1, source_target_pairs={{0,16},{4,20},{8,24},{12,28},{16,0},{20,4},{24,8},{28,12},{1,17},{... | collective-permute-start | bytes 491528 | tf_op jit(solution)/shard_map/ppermute | solution.py:630
  293.0 10.9 %collective-permute-start.38 = (bf16[128,640]{1,0:T(8,128)(2,1)S(1)}, bf16[128,640]{1,0:T(8,128)(2,1)S(1)}, u32[]{:S(2)}, u32[]{:S(2)}) collective-permute-start(bf16[128,640]{1,0:T(8,128)(2,1)S(1)} %copy-done.13), channel_id=1, source_target_pairs={{0,24},{4,28},{8,16},{12,20},{16,8},{20,12},{24,0},{28,4},{1,25},{... | collective-permute-start | bytes 491528 | tf_op jit(solution)/shard_map/ppermute | solution.py:630
  293.2 22.1 %collective-permute-start.24 = (bf16[416,1024]{1,0:T(8,128)(2,1)S(1)}, bf16[416,1024]{1,0:T(8,128)(2,1)S(1)}, u32[]{:S(2)}, u32[]{:S(2)}) collective-permute-start(bf16[416,1024]{1,0:T(8,128)(2,1)S(1)} %add_convert_fusion.2.refs_0_), channel_id=1, source_target_pairs={{0,1},{1,0},{2,3},{3,2},{4,5},{5,4},{6,7},{7,6},{8,9},{9,8},{10,11... | collective-permute-start | bytes 2555912 | tf_op jit(solution)/shard_map/ppermute | solution.py:618
  305.6 8.5 %collective-permute-start.39 = (f32[6,128]{1,0:T(8,128)S(1)}, f32[6,128]{1,0:T(8,128)S(1)}, u32[]{:S(2)}, u32[]{:S(2)}) collective-permute-start(f32[6,128]{1,0:T(8,128)S(1)} %slice.155), channel_id=1, source_target_pairs={{0,1},{1,0},{2,3},{3,2},{4,5},{5,4},{6,7},{7,6},{8,9},{9,8},{10,11... | collective-permute-start | bytes 9224 | tf_op jit(solution)/shard_map/ppermute | solution.py:618
  308.4 9.9 %collective-permute-start.33 = (bf16[128,512]{1,0:T(8,128)(2,1)S(1)}, bf16[128,512]{1,0:T(8,128)(2,1)S(1)}, u32[]{:S(2)}, u32[]{:S(2)}) collective-permute-start(bf16[128,512]{1,0:T(8,128)(2,1)S(1)} %get-tuple-element.174), channel_id=1, source_target_pairs={{0,8},{4,12},{8,0},{12,4},{16,24},{20,28},{24,16},{28,20},{1,9},{5... | collective-permute-start | bytes 393224 | tf_op jit(solution)/shard_map/ppermute | solution.py:630
  310.8 13.2 %collective-permute-start.34 = (bf16[128,512]{1,0:T(8,128)(2,1)S(1)}, bf16[128,512]{1,0:T(8,128)(2,1)S(1)}, u32[]{:S(2)}, u32[]{:S(2)}) collective-permute-start(bf16[128,512]{1,0:T(8,128)(2,1)S(1)} %get-tuple-element.175), channel_id=1, source_target_pairs={{0,16},{4,20},{8,24},{12,28},{16,0},{20,4},{24,8},{28,12},{1,17},{... | collective-permute-start | bytes 393224 | tf_op jit(solution)/shard_map/ppermute | solution.py:630
  314.0 10.0 %collective-permute-start.35 = (bf16[128,512]{1,0:T(8,128)(2,1)S(1)}, bf16[128,512]{1,0:T(8,128)(2,1)S(1)}, u32[]{:S(2)}, u32[]{:S(2)}) collective-permute-start(bf16[128,512]{1,0:T(8,128)(2,1)S(1)} %get-tuple-element.176), channel_id=1, source_target_pairs={{0,24},{4,28},{8,16},{12,20},{16,8},{20,12},{24,0},{28,4},{1,25},{... | collective-permute-start | bytes 393224 | tf_op jit(solution)/shard_map/ppermute | solution.py:630
  (47 other events, 273.9 us)
Sparse Core Ops, SparseCore 0:
  20.4 82.5 all-gather.1
  166.9 94.4 reduce-scatter.1
